TPU v7x, 32 devices: a whole 2x2x4 slice. The times are simulated.
32 devices in a mesh: gx: 4 (over y, x), gy: 8 (over z, core).
Axes of the slice: x: 2, y: 2, z: 4, core: 2. Of those that a mesh axis runs over, the one named last changes fastest.
Arguments:
- selectors: float32 [3, 8, 4, 8, 65536], P(None, None, 'gx', 'gy'), may hold values from 0 to 2047, as said below
- proofs: float32 [3, 8, 4, 8, 65536], P(None, None, 'gx', 'gy'), may hold values from 0 to 2047, as said below
- challenges: int32 [4], replicated, may hold values from 0 to 2147483646
Outputs:
- round_values: float32 [3, 4, 3], replicated
- folded_selectors: float32 [3, 8, 4, 8, 4096], P(None, None, 'gx', 'gy')
- folded_proofs: float32 [3, 8, 4, 8, 4096], P(None, None, 'gx', 'gy')
Inputs may be any that keep to these rules, and one draw needn't show every extreme that they name: `selectors`: limbs of field elements, as in the first step. `proofs`: limbs of field elements, as in the first step. `challenges`: field elements.
All inputs are finite; a program needn't handle non-finite values.
Results may differ from a plain program's by a relative error of at most 0.0003.
Values sent between devices are 32-bit elements; how exact they have to be, the bound alone decides.
No kernel may reach another device: no remote copies, remote signals or barrier semaphores. Data moves between devices by JAX's collectives and lax.ppermute only.
A program may use at most 128 MiB of HBM per device.

v0:
```python
import functools

import jax
import jax.numpy as jnp
from jax import lax
from jax.experimental import pallas as pl
from jax.experimental.pallas import tpu as pltpu
from jax.sharding import PartitionSpec as P


PRIME = 2147483647
LANES = 128
VMEM_ENCODE, VMEM_KERNEL = 16 << 20, 8 << 20


def shr(x, n):
    return lax.shift_right_logical(x, jnp.int32(n))


def reduce_once(x):
    return (x & PRIME) + shr(x, 31)


def add_mod(a, b):
    return reduce_once(a + b)


def sub_mod(a, b):
    return reduce_once(a + (PRIME - b))


def limbs_of(v):
    return v & 2047, shr(v, 11) & 2047, shr(v, 22)


def word_of_limbs(l0, l1, l2):
    half = jnp.floor(l2 * 0.5)
    base = (l0 + l1 * 2048.0) + ((l2 - half * 2.0) * 4194304.0 + 8388608.0)
    negative = half >= 128.0
    scale = jnp.exp2(half - jnp.where(negative, 192.0, 64.0))
    return base * jnp.where(negative, -scale, scale)


def word_of_int(v):
    base = ((v & 8388607) + 8388608).astype(jnp.float32)
    negative = v >= 1073741824
    scale = jnp.exp2(((shr(v, 23) & 127) - 64).astype(jnp.float32))
    return base * jnp.where(negative, -scale, scale)


def int_of_word(x):
    size = jnp.abs(x)
    level = jnp.floor(jnp.log2(size) + 0.0009765625)
    value = size * jnp.exp2(23.0 - level)
    value = jnp.minimum(value, value + value - 8388608.0)
    offset = jnp.where(x < 0.0, jnp.int32((40 << 23) + (1 << 30)), jnp.int32(40 << 23))
    return value.astype(jnp.int32) + (level.astype(jnp.int32) << 23) + offset


def int_of_limbs(l0, l1, l2):
    return (l0 + l1 * 2048.0).astype(jnp.int32) + (l2.astype(jnp.int32) << 22)


def weighted_sum(limbs, weights):
    low = high = None
    for a, c in zip(limbs, weights):
        for n in range(3):
            low = a[n] * c[n] if low is None else low + a[n] * c[n]
            high = a[n] * c[3 + n] if high is None else high + a[n] * c[3 + n]
    return reduce_once(low + ((high & 32767) << 16) + shr(high, 15))


def degrees(a, b):
    return [
        a[0] * b[0],
        a[0] * b[1] + a[1] * b[0],
        a[0] * b[2] + a[1] * b[1] + a[2] * b[0],
        a[1] * b[2] + a[2] * b[1],
        a[2] * b[2],
    ]


def rotate(x, n):
    return ((x << n) & PRIME) + shr(x, 31 - n)


def element_of_degrees(d):
    total = add_mod(reduce_once(d[0]), rotate(d[1], 11))
    total = add_mod(total, rotate(d[2], 22))
    total = add_mod(total, rotate(d[3], 2))
    return add_mod(total, rotate(d[4], 13))


def mul_mod(a, b):
    return element_of_degrees(degrees(limbs_of(a), limbs_of(b)))


def add_limbs(a, b):
    return [x + y for x, y in zip(a, b)]


def nine_of(v):
    s02, s13 = add_limbs(v[0], v[2]), add_limbs(v[1], v[3])
    s01, s23 = add_limbs(v[0], v[1]), add_limbs(v[2], v[3])
    return [*v, s02, s13, s01, s23, add_limbs(s01, s23)]


def clear(acc_ref):
    for n in range(45):
        acc_ref[n] = jnp.zeros((8, LANES), jnp.int32)


def two_rounds(acc_ref, splat_ref, s, w):
    s, w = [[limbs_of(x) for x in v] for v in (s, w)]
    for kind, (a, b) in enumerate(zip(nine_of(s), nine_of(w))):
        for n, d in enumerate(degrees(a, b)):
            acc_ref[5 * kind + n] = acc_ref[5 * kind + n] + d
    weights = [[splat_ref[6 * x + n] for n in range(6)] for x in range(4)]
    return weighted_sum(s, weights), weighted_sum(w, weights)


def flush(acc_ref, points_ref, first):
    for kind in range(9):
        here = element_of_degrees([acc_ref[5 * kind + n] for n in range(5)])
        points_ref[first + kind] = add_mod(points_ref[first + kind], here)


def whole(scalar):
    return jnp.full((8, LANES), scalar, jnp.int32)


def sides(challenges_ref, place, phase):
    out = []
    for k in range(2):
        high = whole(challenges_ref[2 * phase + k])
        low = jnp.where(high == 0, 1, PRIME - high + 1)
        is_low = whole((place >> (1 - k)) & 1) == 0
        out.append((jnp.where(is_low, low, high), jnp.where(is_low, high, low)))
    return out


def constants_of(weight):
    parts = [weight, rotate(weight, 11), rotate(weight, 22)]
    return [x & 65535 for x in parts] + [shr(x, 16) for x in parts]


def splat_weights(challenges_ref, place, phase, splat_ref):
    first, second = sides(challenges_ref, place, phase)
    for x in range(4):
        for n, c in enumerate(constants_of(mul_mod(first[x >> 1], second[x & 1]))):
            splat_ref[6 * x + n] = c


def tile(start, i):
    return pl.ds(pl.multiple_of(start + i * 8, 8), 8)


def encode_kernel(start, place_ref, s_hbm, w_hbm, *refs):
    own_ref, o1, o2, o3, token_ref, buffer, sems = refs[-7:]
    count, rows = own_ref.shape[1], own_ref.shape[2]
    here = place_ref[0]
    order = [(j, d, t) for j in range(count) for d in (1, 2, 3, 0) for t in range(2)]

    def copy(j, d, t):
        src = (s_hbm, w_hbm)[t].at[:, start + j, pl.ds(pl.multiple_of((here ^ d) * rows, rows), rows), :]
        return pltpu.make_async_copy(src, buffer.at[j, d, t], sems.at[j, d, t])

    for where in order:
        copy(*where).start()
    token_ref[...] = jnp.zeros_like(token_ref)
    for where in order:
        j, d, t = where
        copy(*where).wait()

        def step(i, _):
            at = tile(0, i)
            limbs = [buffer[j, d, t, n, at] for n in range(3)]
            if d:
                (o1, o2, o3)[d - 1][t, j, at] = word_of_limbs(*limbs)
            else:
                own_ref[t, j, at] = int_of_limbs(*limbs)

        lax.fori_loop(0, rows // 8, step, None, unroll=4)


def first_kernel(fresh, challenges_ref, gx_ref, gy_ref, own_ref, g1, g2, g3, *refs):
    if not fresh:
        before_ref, *refs = refs
    points_ref, kept_ref, o1, o2, o3, acc_ref, splat_ref = refs
    count, rows = own_ref.shape[1], own_ref.shape[2]
    sub = rows // 4
    given, outs = (g1, g2, g3), (kept_ref, o1, o2, o3)
    splat_weights(challenges_ref, gx_ref[0], 0, splat_ref)
    points_ref[...] = jnp.zeros_like(points_ref) if fresh else before_ref[...]

    def pair(j, _):
        clear(acc_ref)
        for e in range(4):
            start = (gy_ref[0] ^ e) * sub

            def step(i, _):
                at = tile(start, i)
                s, w = [[own_ref[t, j, at]] + [int_of_word(g[t, j, at]) for g in given] for t in range(2)]
                for t, folded in enumerate(two_rounds(acc_ref, splat_ref, s, w)):
                    outs[e][t, j, tile(0, i)] = word_of_int(folded) if e else folded

            lax.fori_loop(0, sub // 8, step, None, unroll=2)
        flush(acc_ref, points_ref, 0)

    lax.fori_loop(0, count, pair, None)


def settle(lowest, middle, highest):
    for _ in range(3):
        carried = jnp.floor(lowest * (1.0 / 2048.0))
        lowest = lowest - carried * 2048.0
        middle = middle + carried
        carried = jnp.floor(middle * (1.0 / 2048.0))
        middle = middle - carried * 2048.0
        highest = highest + carried
        carried = jnp.floor(highest * (1.0 / 512.0))
        highest = highest - carried * 512.0
        lowest = lowest + carried
    at_modulus = (lowest == 2047.0) & (middle == 2047.0) & (highest == 511.0)
    return [jnp.where(at_modulus, 0.0, limb) for limb in (lowest, middle, highest)]


def round_sums(challenges_ref, place, phase, points):
    own, other = sides(challenges_ref, place, phase)[0]
    squares = [constants_of(mul_mod(*x)) for x in ((own, own), (own, other), (other, other))]
    i0, i1, i2, i3, i02, i13, i01, i23, i0123 = points
    first = [add_mod(i0, i1), add_mod(i2, i3), add_mod(i02, i13)]
    second = []
    for own, other, both in ((i0, i2, i02), (i1, i3, i13), (i01, i23, i0123)):
        cross = sub_mod(both, add_mod(own, other))
        second.append(weighted_sum([limbs_of(x) for x in (own, cross, other)], squares))
    return [first, second]


def publish_row(challenges_ref, places, points_ref, sums_ref):
    lane = lax.broadcasted_iota(jnp.int32, (1, LANES), 1)
    rows = [jnp.zeros((1, LANES), jnp.float32) for _ in range(3)]
    for phase in range(2):
        place = places[phase]
        points = [points_ref[9 * phase + n] for n in range(9)]
        for k, (own, other, both) in enumerate(round_sums(challenges_ref, place, phase, points)):
            is_low = whole((place >> (1 - k)) & 1) == 0
            at_zero = jnp.where(is_low, own, other)
            at_one = jnp.where(is_low, other, own)
            once = add_mod(at_zero, add_mod(at_one, at_one))
            at_two = sub_mod(add_mod(once, add_mod(once, once)), add_mod(both, both))
            for t, value in enumerate((at_zero, at_one, at_two)):
                for n, limb in enumerate(limbs_of(value)):
                    total = jnp.sum(limb.astype(jnp.float32), axis=(0, 1), keepdims=True)
                    rows[n] = jnp.where(lane == 6 * phase + 3 * k + t, total, rows[n])
    low, mid, high = settle(*rows)
    packed = low + pltpu.roll(mid, 16, 1) + pltpu.roll(high, 32, 1)
    sums_ref[...] = jnp.broadcast_to(packed, sums_ref.shape)


def second_kernel(start, fresh, last, challenges_ref, gx_ref, gy_ref, kept_ref, g1, g2, g3, before_ref, *refs):
    if not fresh:
        refs = refs[2:]
    points_ref, s_ref, w_ref, *refs = refs
    if last:
        sums_ref, s_hbm, w_hbm, *refs = refs
        sems = refs.pop()
    acc_ref, splat_ref = refs
    count, rows = kept_ref.shape[1], kept_ref.shape[2]
    given = (g1, g2, g3)

    def copies(which, part):
        return [
            pltpu.make_async_copy(src.at[:, part], dst.at[:, part], sems.at[which, t])
            for t, (src, dst) in enumerate(((s_ref, s_hbm), (w_ref, w_hbm)))
        ]

    if last and start:
        for copy in copies(0, pl.ds(0, start)):
            copy.start()
    splat_weights(challenges_ref, gy_ref[0], 1, splat_ref)
    points_ref[...] = before_ref[...]

    def pair(j, _):
        clear(acc_ref)

        def step(i, _):
            at = tile(0, i)
            s, w = [[kept_ref[t, j, at]] + [int_of_word(g[t, j, at]) for g in given] for t in range(2)]
            for out, folded in zip((s_ref, w_ref), two_rounds(acc_ref, splat_ref, s, w)):
                for n, limb in enumerate(limbs_of(jnp.where(folded == PRIME, 0, folded))):
                    out[n, start + j, at] = limb.astype(jnp.float32)

        lax.fori_loop(0, rows // 8, step, None, unroll=2)
        flush(acc_ref, points_ref, 9)

    lax.fori_loop(0, count, pair, None)
    if last:
        for copy in copies(1, pl.ds(start, count)):
            copy.start()
        publish_row(challenges_ref, (gx_ref[0], gy_ref[0]), points_ref, sums_ref)
        for copy in copies(1, pl.ds(start, count)) + (copies(0, pl.ds(0, start)) if start else []):
            copy.wait()


def swap_with(x, axis, mask):
    return lax.ppermute(x, axis, [(i, i ^ mask) for i in range(lax.axis_size(axis))])


CHUNKS = (3, 3, 2)
POINTS = pltpu.VMEM((18, 8, LANES), jnp.int32)


def shards(devices, selectors, proofs, challenges):
    polynomials, row_count = selectors.shape[1], selectors.shape[-1]
    lane_rows = row_count // LANES
    quarter, final = lane_rows // 4, lane_rows // 16
    tables = [
        pltpu.with_memory_space_constraint(x.reshape(3, polynomials, lane_rows, LANES), pltpu.HBM)
        for x in (selectors, proofs)
    ]
    gx_shift = lax.axis_size("gx").bit_length() - 3
    gy_shift = lax.axis_size("gy").bit_length() - 3
    gx_place = (lax.axis_index("gx") >> gx_shift).astype(jnp.int32).reshape(1)
    gy_place = (lax.axis_index("gy") >> gy_shift).astype(jnp.int32).reshape(1)

    sizes = CHUNKS if sum(CHUNKS) == polynomials else (1,) * polynomials
    starts = [sum(sizes[:c]) for c in range(len(sizes))]
    chunks = len(sizes)
    smem, vmem, hbm, anywhere = [pl.BlockSpec(memory_space=m) for m in (pltpu.SMEM, pltpu.VMEM, pltpu.HBM, pl.ANY)]

    def words(count, rows, dtype=jnp.float32):
        return pltpu.VMEM((2, count, rows, LANES), dtype)

    def near(arrays):
        return [pltpu.with_memory_space_constraint(x, pltpu.VMEM) for x in arrays]

    work = [pltpu.VMEM((45, 8, LANES), jnp.int32), pltpu.VMEM((24, 8, LANES), jnp.int32)]
    small = pltpu.CompilerParams(vmem_limit_bytes=VMEM_KERNEL)

    def encode(c, token):
        count = sizes[c]
        return pl.pallas_call(
            functools.partial(encode_kernel, starts[c]),
            in_specs=[smem, hbm, hbm] + [anywhere] * len(token),
            out_specs=[vmem] * 5,
            out_shape=[words(count, quarter, jnp.int32)] + [words(count, quarter)] * 3
            + [pltpu.VMEM((8, LANES), jnp.float32)],
            scratch_shapes=[
                pltpu.VMEM((count, 4, 2, 3, quarter, LANES), jnp.float32),
                pltpu.SemaphoreType.DMA((count, 4, 2)),
            ],
            compiler_params=pltpu.CompilerParams(vmem_limit_bytes=VMEM_ENCODE),
            name="encode",
        )(gx_place, *tables, *token)

    def first(c, own, given, before):
        count = sizes[c]
        fresh = before is None
        return pl.pallas_call(
            functools.partial(first_kernel, fresh),
            in_specs=[smem] * 3 + [vmem] * (4 if fresh else 5),
            out_specs=[vmem] * 5,
            out_shape=[POINTS, words(count, final, jnp.int32)] + [words(count, final)] * 3,
            scratch_shapes=work,
            input_output_aliases={} if fresh else {7: 0},
            compiler_params=small,
            name="first_rounds",
        )(challenges, gx_place, gy_place, own, *near(given), *(() if fresh else (before,)))

    def second(c, kept, given, before, folded):
        fresh, last = folded is None, c == chunks - 1
        shape = (3, polynomials, final, LANES)
        out_shape, out_specs = [POINTS] + [pltpu.VMEM(shape, jnp.float32)] * 2, [vmem] * 3
        scratch = list(work)
        if last:
            out_shape += [jax.ShapeDtypeStruct((devices, 1, LANES), jnp.float32)] + [jax.ShapeDtypeStruct(shape, jnp.float32)] * 2
            out_specs += [vmem, hbm, hbm]
            scratch.append(pltpu.SemaphoreType.DMA((2, 2)))
        return pl.pallas_call(
            functools.partial(second_kernel, starts[c], fresh, last),
            in_specs=[smem] * 3 + [vmem] * (5 if fresh else 7),
            out_specs=out_specs,
            out_shape=out_shape,
            scratch_shapes=scratch,
            input_output_aliases={7: 0} if fresh else {7: 0, 8: 1, 9: 2},
            compiler_params=small,
            name="second_rounds",
        )(challenges, gx_place, gy_place, kept, *near(given), before, *(() if fresh else folded))

    owns, sent = [], []
    token = []
    chunks = len(sizes)
    for c in range(chunks):
        own, *given, token = encode(c, token)
        token = [token]
        owns.append(own)
        sent.append([swap_with(x, "gx", (d + 1) << gx_shift) for d, x in enumerate(given)])
    points, folded, waiting = None, None, []
    for c in range(chunks + 1):
        if c < chunks:
            points, kept, *given = first(c, owns[c], sent[c], points)
            waiting.append((kept, [swap_with(x, "gy", (e + 1) << gy_shift) for e, x in enumerate(given)]))
        if c:
            points, *folded = second(c - 1, *waiting[c - 1], points, folded)
    sums, *folded = folded[2:]
    gathered = lax.all_to_all(sums, ("gx", "gy"), 0, 0)
    total = gathered.sum(axis=0).reshape(LANES)
    points = jnp.stack(settle(total[0:12], total[16:28], total[32:44])).reshape(3, 4, 3)
    shape = (3, polynomials, 1, 1, row_count // 16)
    return points, folded[0].reshape(shape), folded[1].reshape(shape)


def solution(mesh):
    tables = P(None, None, "gx", "gy", None)
    devices = mesh.shape["gx"] * mesh.shape["gy"]

    def body(*arrays):
        return shards(devices, *arrays)

    return jax.shard_map(
        body,
        mesh=mesh,
        in_specs=(tables, tables, P()),
        out_specs=(P(), tables, tables),
        check_vma=False,
    )
```

profile of v0, /device:TPU:0, one launch (start us, length us, event | category | flops | bytes accessed | tf_op | source)
XLA Modules:
  0.0 99.0 jit_solution(9027982090641528903)
XLA Ops:
  0.6 2.7 %encode.3 = (s32[2,3,128,128]{3,2,1,0:T(8,128)S(1)}, f32[2,3,128,128]{3,2,1,0:T(8,128)S(1)}, f32[2,3,128,128]{3,2,1,0:T(8,128)S(1)}, f32[2,3,128,128]{3,2,1,0:T(8,128)S(1)}, f32[8,128]{1,0:T(8,128)S(1)}) custom-call(s32[1]{0:T(128)} %bitcast.place_ref.gx_ref, f32[3,8,512,128]{3,2,1,0:T(8,128)} %bitcast.7, f32[3,8,512,128]{3,2,1,0:T(8,128)} %bitcast.10), custom_call_target="tpu_custom_call" | custom-call | tf_op jit(solution)/shard_map/encode/pallas_call | solution.py:343
  3.3 3.0 %collective-permute-start.3 = (f32[2,3,128,128]{3,2,1,0:T(8,128)S(1)}, f32[2,3,128,128]{3,2,1,0:T(8,128)S(1)}, u32[]{:S(2)}, u32[]{:S(2)}) collective-permute-start(f32[2,3,128,128]{3,2,1,0:T(8,128)S(1)} %get-tuple-element.48), channel_id=1, source_target_pairs={{0,8},{8,0},{16,24},{24,16},{1,9},{9,1},{17,25},{25,17},{2,10},{10... | collective-permute-start | bytes 1179656 | tf_op jit(solution)/shard_map/ppermute | solution.py:307
  6.4 3.7 %encode.4 = (s32[2,3,128,128]{3,2,1,0:T(8,128)S(1)}, f32[2,3,128,128]{3,2,1,0:T(8,128)}, f32[2,3,128,128]{3,2,1,0:T(8,128)}, f32[2,3,128,128]{3,2,1,0:T(8,128)}, f32[8,128]{1,0:T(8,128)S(1)}) custom-call(s32[1]{0:T(128)} %bitcast.place_ref.gx_ref, f32[3,8,512,128]{3,2,1,0:T(8,128)} %bitcast.8, f32[3,8,512,128]{3,2,1,0:T(8,128)} %bitcast.11, ...), custom_call_target="tpu_custom_call" | custom-call | tf_op jit(solution)/shard_map/encode/pallas_call | solution.py:343
  10.0 0.0 copy-start.2
  10.1 2.9 %encode.5 = (s32[2,2,128,128]{3,2,1,0:T(8,128)S(1)}, f32[2,2,128,128]{3,2,1,0:T(8,128)S(1)}, f32[2,2,128,128]{3,2,1,0:T(8,128)}, f32[2,2,128,128]{3,2,1,0:T(8,128)}, f32[8,128]{1,0:T(8,128)}) custom-call(s32[1]{0:T(128)} %bitcast.place_ref.gx_ref, f32[3,8,512,128]{3,2,1,0:T(8,128)} %bitcast.9, f32[3,8,512,128]{3,2,1,0:T(8,128)} %bitcast.12, ...), custom_call_target="tpu_custom_call" | custom-call | tf_op jit(solution)/shard_map/encode/pallas_call | solution.py:343
  13.0 0.1 collective-permute-start
  13.1 2.0 %collective-permute-start.4 = (f32[2,3,128,128]{3,2,1,0:T(8,128)S(1)}, f32[2,3,128,128]{3,2,1,0:T(8,128)S(1)}, u32[]{:S(2)}, u32[]{:S(2)}) collective-permute-start(f32[2,3,128,128]{3,2,1,0:T(8,128)S(1)} %get-tuple-element.49), channel_id=1, source_target_pairs={{0,16},{8,24},{16,0},{24,8},{1,17},{9,25},{17,1},{25,9},{2,18},{10... | collective-permute-start | bytes 1179656 | tf_op jit(solution)/shard_map/ppermute | solution.py:307
  15.1 1.4 %collective-permute-start.5 = (f32[2,3,128,128]{3,2,1,0:T(8,128)S(1)}, f32[2,3,128,128]{3,2,1,0:T(8,128)S(1)}, u32[]{:S(2)}, u32[]{:S(2)}) collective-permute-start(f32[2,3,128,128]{3,2,1,0:T(8,128)S(1)} %get-tuple-element.50), channel_id=1, source_target_pairs={{0,24},{8,16},{16,8},{24,0},{1,25},{9,17},{17,9},{25,1},{2,26},{10... | collective-permute-start | bytes 1179656 | tf_op jit(solution)/shard_map/ppermute | solution.py:307
  16.6 0.1 collective-permute-start.9
  16.6 5.6 %collective-permute-done.g1 = f32[2,2,128,128]{3,2,1,0:T(8,128)S(1)} collective-permute-done((f32[2,2,128,128]{3,2,1,0:T(8,128)S(1)}, f32[2,2,128,128]{3,2,1,0:T(8,128)S(1)}, u32[]{:S(2)}, u32[]{:S(2)}) %collective-permute-start) | collective-permute-done | bytes 262176 | tf_op jit(solution)/shard_map/ppermute | solution.py:307
  22.3 0.7 copy-done
  23.0 1.5 %collective-permute-start.10 = (f32[2,3,128,128]{3,2,1,0:T(8,128)}, f32[2,3,128,128]{3,2,1,0:T(8,128)S(1)}, u32[]{:S(2)}, u32[]{:S(2)}) collective-permute-start(f32[2,3,128,128]{3,2,1,0:T(8,128)} %get-tuple-element.57), channel_id=1, source_target_pairs={{0,16},{8,24},{16,0},{24,8},{1,17},{9,25},{17,1},{25,9},{2,18},{10... | collective-permute-start | bytes 1179656 | tf_op jit(solution)/shard_map/ppermute | solution.py:307
  24.5 1.7 %collective-permute-start.11 = (f32[2,3,128,128]{3,2,1,0:T(8,128)}, f32[2,3,128,128]{3,2,1,0:T(8,128)S(1)}, u32[]{:S(2)}, u32[]{:S(2)}) collective-permute-start(f32[2,3,128,128]{3,2,1,0:T(8,128)} %get-tuple-element.58), channel_id=1, source_target_pairs={{0,24},{8,16},{16,8},{24,0},{1,25},{9,17},{17,9},{25,1},{2,26},{10... | collective-permute-start | bytes 1179656 | tf_op jit(solution)/shard_map/ppermute | solution.py:307
  26.1 7.3 %collective-permute-done.4.g2 = f32[2,3,128,128]{3,2,1,0:T(8,128)S(1)} collective-permute-done((f32[2,3,128,128]{3,2,1,0:T(8,128)S(1)}, f32[2,3,128,128]{3,2,1,0:T(8,128)S(1)}, u32[]{:S(2)}, u32[]{:S(2)}) %collective-permute-start.4) | collective-permute-done | bytes 393248 | tf_op jit(solution)/shard_map/ppermute | solution.py:307
  33.5 2.1 %collective-permute-start.1 = (f32[2,2,128,128]{3,2,1,0:T(8,128)}, f32[2,2,128,128]{3,2,1,0:T(8,128)}, u32[]{:S(2)}, u32[]{:S(2)}) collective-permute-start(f32[2,2,128,128]{3,2,1,0:T(8,128)} %get-tuple-element.45), channel_id=1, source_target_pairs={{0,16},{8,24},{16,0},{24,8},{1,17},{9,25},{17,1},{25,9},{2,18},{10... | collective-permute-start | bytes 786440 | tf_op jit(solution)/shard_map/ppermute | solution.py:307
  35.5 1.2 %collective-permute-start.2 = (f32[2,2,128,128]{3,2,1,0:T(8,128)}, f32[2,2,128,128]{3,2,1,0:T(8,128)}, u32[]{:S(2)}, u32[]{:S(2)}) collective-permute-start(f32[2,2,128,128]{3,2,1,0:T(8,128)} %get-tuple-element.46), channel_id=1, source_target_pairs={{0,24},{8,16},{16,8},{24,0},{1,25},{9,17},{17,9},{25,1},{2,26},{10... | collective-permute-start | bytes 786440 | tf_op jit(solution)/shard_map/ppermute | solution.py:307
  36.8 4.3 %first_rounds.3 = (s32[18,8,128]{2,1,0:T(8,128)S(1)}, s32[2,3,32,128]{3,2,1,0:T(8,128)S(1)}, f32[2,3,32,128]{3,2,1,0:T(8,128)S(1)}, f32[2,3,32,128]{3,2,1,0:T(8,128)S(1)}, f32[2,3,32,128]{3,2,1,0:T(8,128)S(1)}) custom-call(s32[4]{0:T(128)S(1)} %copy-done.2, s32[1]{0:T(128)} %bitcast.place_ref.gx_ref, s32[1]{0:T(128)} %bitcast.1.gy_ref, ...), custom_call_target="tpu_custom_call" | custom-call | tf_op jit(solution)/shard_map/first_rounds/pallas_call | solution.py:360
  41.1 0.0 collective-permute-done.9.g1
  41.1 1.6 %collective-permute-start.6 = (f32[2,3,32,128]{3,2,1,0:T(8,128)S(1)}, f32[2,3,32,128]{3,2,1,0:T(8,128)S(1)}, u32[]{:S(2)}, u32[]{:S(2)}) collective-permute-start(f32[2,3,32,128]{3,2,1,0:T(8,128)S(1)} %get-tuple-element.52), channel_id=1, source_target_pairs={{0,2},{1,3},{2,0},{3,1},{4,6},{5,7},{6,4},{7,5},{8,10},{9,11},{10,... | collective-permute-start | bytes 294920 | tf_op jit(solution)/shard_map/ppermute | solution.py:307
  42.7 13.2 %collective-permute-done.10.g2 = f32[2,3,128,128]{3,2,1,0:T(8,128)S(1)} collective-permute-done((f32[2,3,128,128]{3,2,1,0:T(8,128)}, f32[2,3,128,128]{3,2,1,0:T(8,128)S(1)}, u32[]{:S(2)}, u32[]{:S(2)}) %collective-permute-start.10) | collective-permute-done | bytes 393248 | tf_op jit(solution)/shard_map/ppermute | solution.py:307
  56.0 2.9 %collective-permute-start.7 = (f32[2,3,32,128]{3,2,1,0:T(8,128)S(1)}, f32[2,3,32,128]{3,2,1,0:T(8,128)S(1)}, u32[]{:S(2)}, u32[]{:S(2)}) collective-permute-start(f32[2,3,32,128]{3,2,1,0:T(8,128)S(1)} %get-tuple-element.53), channel_id=1, source_target_pairs={{0,4},{1,5},{2,6},{3,7},{4,0},{5,1},{6,2},{7,3},{8,12},{9,13},{10,... | collective-permute-start | bytes 294920 | tf_op jit(solution)/shard_map/ppermute | solution.py:307
  58.9 1.3 %collective-permute-start.8 = (f32[2,3,32,128]{3,2,1,0:T(8,128)S(1)}, f32[2,3,32,128]{3,2,1,0:T(8,128)S(1)}, u32[]{:S(2)}, u32[]{:S(2)}) collective-permute-start(f32[2,3,32,128]{3,2,1,0:T(8,128)S(1)} %get-tuple-element.54), channel_id=1, source_target_pairs={{0,6},{1,7},{2,4},{3,5},{4,2},{5,3},{6,0},{7,1},{8,14},{9,15},{10,... | collective-permute-start | bytes 294920 | tf_op jit(solution)/shard_map/ppermute | solution.py:307
  60.3 4.3 %first_rounds.4 = (s32[18,8,128]{2,1,0:T(8,128)S(1)}, s32[2,3,32,128]{3,2,1,0:T(8,128)S(1)}, f32[2,3,32,128]{3,2,1,0:T(8,128)S(1)}, f32[2,3,32,128]{3,2,1,0:T(8,128)S(1)}, f32[2,3,32,128]{3,2,1,0:T(8,128)S(1)}) custom-call(s32[4]{0:T(128)S(1)} %copy-done.2, s32[1]{0:T(128)} %bitcast.place_ref.gx_ref, ...), custom_call_target="tpu_custom_call", output_to_operand_aliasing={{0}: (7, {})} | custom-call | tf_op jit(solution)/shard_map/first_rounds/pallas_call | solution.py:360
  64.6 0.0 collective-permute-done.6.g1
  64.6 0.3 collective-permute-start.15
  64.9 2.8 %collective-permute-start.16 = (f32[2,3,32,128]{3,2,1,0:T(8,128)S(1)}, f32[2,3,32,128]{3,2,1,0:T(8,128)S(1)}, u32[]{:S(2)}, u32[]{:S(2)}) collective-permute-start(f32[2,3,32,128]{3,2,1,0:T(8,128)S(1)} %get-tuple-element.68), channel_id=1, source_target_pairs={{0,4},{1,5},{2,6},{3,7},{4,0},{5,1},{6,2},{7,3},{8,12},{9,13},{10,... | collective-permute-start | bytes 294920 | tf_op jit(solution)/shard_map/ppermute | solution.py:307
  67.7 2.2 %collective-permute-start.17 = (f32[2,3,32,128]{3,2,1,0:T(8,128)S(1)}, f32[2,3,32,128]{3,2,1,0:T(8,128)S(1)}, u32[]{:S(2)}, u32[]{:S(2)}) collective-permute-start(f32[2,3,32,128]{3,2,1,0:T(8,128)S(1)} %get-tuple-element.69), channel_id=1, source_target_pairs={{0,6},{1,7},{2,4},{3,5},{4,2},{5,3},{6,0},{7,1},{8,14},{9,15},{10,... | collective-permute-start | bytes 294920 | tf_op jit(solution)/shard_map/ppermute | solution.py:307
  69.9 1.6 %second_rounds.3 = (s32[18,8,128]{2,1,0:T(8,128)S(1)}, f32[3,8,32,128]{3,2,1,0:T(8,128)S(1)}, f32[3,8,32,128]{3,2,1,0:T(8,128)S(1)}) custom-call(s32[4]{0:T(128)S(1)} %copy-done.2, s32[1]{0:T(128)} %bitcast.place_ref.gx_ref, s32[1]{0:T(128)} %bitcast.1.gy_ref, s32[2,3,32,128]{3,2,1,0:T(8,128)S(1)} %get-tuple-element.51.kept_ref, ...), custom_call_target="tpu_custom_call", output_to_operand_aliasing={{0}: (7, {})} | custom-call | tf_op jit(solution)/shard_map/second_rounds/pallas_call | solution.py:380
  71.5 0.0 collective-permute-done.1.g2
  71.5 0.0 collective-permute-done.2.g3
  71.6 0.9 copy-done.1
  72.5 3.6 %first_rounds.5 = (s32[18,8,128]{2,1,0:T(8,128)S(1)}, s32[2,2,32,128]{3,2,1,0:T(8,128)S(1)}, f32[2,2,32,128]{3,2,1,0:T(8,128)S(1)}, f32[2,2,32,128]{3,2,1,0:T(8,128)S(1)}, f32[2,2,32,128]{3,2,1,0:T(8,128)S(1)}) custom-call(s32[4]{0:T(128)S(1)} %copy-done.2, s32[1]{0:T(128)} %bitcast.place_ref.gx_ref, ...), custom_call_target="tpu_custom_call", output_to_operand_aliasing={{0}: (7, {})} | custom-call | tf_op jit(solution)/shard_map/first_rounds/pallas_call | solution.py:360
  76.1 1.8 %collective-permute-start.12 = (f32[2,2,32,128]{3,2,1,0:T(8,128)S(1)}, f32[2,2,32,128]{3,2,1,0:T(8,128)S(1)}, u32[]{:S(2)}, u32[]{:S(2)}) collective-permute-start(f32[2,2,32,128]{3,2,1,0:T(8,128)S(1)} %get-tuple-element.63), channel_id=1, source_target_pairs={{0,2},{1,3},{2,0},{3,1},{4,6},{5,7},{6,4},{7,5},{8,10},{9,11},{10,... | collective-permute-start | bytes 196616 | tf_op jit(solution)/shard_map/ppermute | solution.py:307
  77.9 0.4 collective-permute-start.13
  78.3 0.0 collective-permute-done.15.g1
  78.3 2.2 %collective-permute-start.14 = (f32[2,2,32,128]{3,2,1,0:T(8,128)S(1)}, f32[2,2,32,128]{3,2,1,0:T(8,128)S(1)}, u32[]{:S(2)}, u32[]{:S(2)}) collective-permute-start(f32[2,2,32,128]{3,2,1,0:T(8,128)S(1)} %get-tuple-element.65), channel_id=1, source_target_pairs={{0,6},{1,7},{2,4},{3,5},{4,2},{5,3},{6,0},{7,1},{8,14},{9,15},{10,... | collective-permute-start | bytes 196616 | tf_op jit(solution)/shard_map/ppermute | solution.py:307
  80.5 1.6 %second_rounds.4 = (s32[18,8,128]{2,1,0:T(8,128)S(1)}, f32[3,8,32,128]{3,2,1,0:T(8,128)S(1)}, f32[3,8,32,128]{3,2,1,0:T(8,128)S(1)}) custom-call(s32[4]{0:T(128)S(1)} %copy-done.2, s32[1]{0:T(128)} %bitcast.place_ref.gx_ref, s32[1]{0:T(128)} %bitcast.1.gy_ref, ...), custom_call_target="tpu_custom_call", output_to_operand_aliasing={{0}: (7, {}), {1}: (8, {}), {2}: (9, {})} | custom-call | tf_op jit(solution)/shard_map/second_rounds/pallas_call | solution.py:380
  82.2 1.3 %collective-permute-done.13.g2 = f32[2,2,32,128]{3,2,1,0:T(8,128)S(1)} collective-permute-done((f32[2,2,32,128]{3,2,1,0:T(8,128)S(1)}, f32[2,2,32,128]{3,2,1,0:T(8,128)S(1)}, u32[]{:S(2)}, u32[]{:S(2)}) %collective-permute-start.13) | collective-permute-done | bytes 65568 | tf_op jit(solution)/shard_map/ppermute | solution.py:307
  83.5 1.0 %collective-permute-done.14.g3 = f32[2,2,32,128]{3,2,1,0:T(8,128)S(1)} collective-permute-done((f32[2,2,32,128]{3,2,1,0:T(8,128)S(1)}, f32[2,2,32,128]{3,2,1,0:T(8,128)S(1)}, u32[]{:S(2)}, u32[]{:S(2)}) %collective-permute-start.14) | collective-permute-done | bytes 65568 | tf_op jit(solution)/shard_map/ppermute | solution.py:307
  84.5 2.3 %second_rounds.5 = (s32[18,8,128]{2,1,0:T(8,128)S(1)}, f32[3,8,32,128]{3,2,1,0:T(8,128)S(1)}, f32[3,8,32,128]{3,2,1,0:T(8,128)S(1)}, f32[32,1,128]{2,1,0:T(1,128...) custom-call(s32[4]{0:T(128)S(1)} %copy-done.2, ...), custom_call_target="tpu_custom_call", output_to_operand_aliasing={{0}: (7, {}), {1}: (8, {}), {2}: (9, {})} | custom-call | tf_op jit(solution)/shard_map/second_rounds/pallas_call | solution.py:380
  86.7 11.1 %all_to_all.5 = f32[32,1,128]{2,1,0:T(1,128)S(1)} all-to-all(f32[32,1,128]{2,1,0:T(1,128)S(1)} %get-tuple-element.76), channel_id=1, replica_groups=mesh['gx'=4,'gy'=8] {'gx','gy'}, dimensions={0} | all-to-all | bytes 32768 | tf_op jit(solution)/shard_map/all_to_all | solution.py:407
  97.9 0.1 reduce_sum.11
  97.9 0.1 subtract_add_fusion.6
  98.0 0.1 subtract_add_fusion.5
  98.1 0.1 stack.12
  98.2 0.1 stack.14
  98.3 0.1 stack.13
  98.4 0.6 pad_maximum_fusion
  (13 shorter events, 0.1 us)
Async XLA Ops:
  3.3 21.2 %collective-permute-start.3 = (f32[2,3,128,128]{3,2,1,0:T(8,128)S(1)}, f32[2,3,128,128]{3,2,1,0:T(8,128)S(1)}, u32[]{:S(2)}, u32[]{:S(2)}) collective-permute-start(f32[2,3,128,128]{3,2,1,0:T(8,128)S(1)} %get-tuple-element.48), channel_id=1, source_target_pairs={{0,8},{8,0},{16,24},{24,16},{1,9},{9,1},{17,25},{25,17},{2,10},{10... | collective-permute-start | bytes 1179656 | tf_op jit(solution)/shard_map/ppermute | solution.py:307
  10.0 26.8 %copy-start.2 = (s32[4]{0:T(128)S(1)}, s32[4]{0:T(128)}, u32[]{:S(2)}) copy-start(s32[4]{0:T(128)} %challenges_ref.11) | copy-start | bytes 52
  13.0 9.2 %collective-permute-start = (f32[2,2,128,128]{3,2,1,0:T(8,128)S(1)}, f32[2,2,128,128]{3,2,1,0:T(8,128)S(1)}, u32[]{:S(2)}, u32[]{:S(2)}) collective-permute-start(f32[2,2,128,128]{3,2,1,0:T(8,128)S(1)} %get-tuple-element.44), channel_id=1, source_target_pairs={{0,8},{8,0},{16,24},{24,16},{1,9},{9,1},{17,25},{25,17},{2,10},{10... | collective-permute-start | bytes 786440 | tf_op jit(solution)/shard_map/ppermute | solution.py:307
  13.1 20.4 %collective-permute-start.4 = (f32[2,3,128,128]{3,2,1,0:T(8,128)S(1)}, f32[2,3,128,128]{3,2,1,0:T(8,128)S(1)}, u32[]{:S(2)}, u32[]{:S(2)}) collective-permute-start(f32[2,3,128,128]{3,2,1,0:T(8,128)S(1)} %get-tuple-element.49), channel_id=1, source_target_pairs={{0,16},{8,24},{16,0},{24,8},{1,17},{9,25},{17,1},{25,9},{2,18},{10... | collective-permute-start | bytes 1179656 | tf_op jit(solution)/shard_map/ppermute | solution.py:307
  15.1 20.4 %collective-permute-start.5 = (f32[2,3,128,128]{3,2,1,0:T(8,128)S(1)}, f32[2,3,128,128]{3,2,1,0:T(8,128)S(1)}, u32[]{:S(2)}, u32[]{:S(2)}) collective-permute-start(f32[2,3,128,128]{3,2,1,0:T(8,128)S(1)} %get-tuple-element.50), channel_id=1, source_target_pairs={{0,24},{8,16},{16,8},{24,0},{1,25},{9,17},{17,9},{25,1},{2,26},{10... | collective-permute-start | bytes 1179656 | tf_op jit(solution)/shard_map/ppermute | solution.py:307
  16.6 24.5 %collective-permute-start.9 = (f32[2,3,128,128]{3,2,1,0:T(8,128)}, f32[2,3,128,128]{3,2,1,0:T(8,128)S(1)}, u32[]{:S(2)}, u32[]{:S(2)}) collective-permute-start(f32[2,3,128,128]{3,2,1,0:T(8,128)} %get-tuple-element.56), channel_id=1, source_target_pairs={{0,8},{8,0},{16,24},{24,16},{1,9},{9,1},{17,25},{25,17},{2,10},{10... | collective-permute-start | bytes 1179656 | tf_op jit(solution)/shard_map/ppermute | solution.py:307
  22.3 0.7 copy-start
  23.0 33.0 %collective-permute-start.10 = (f32[2,3,128,128]{3,2,1,0:T(8,128)}, f32[2,3,128,128]{3,2,1,0:T(8,128)S(1)}, u32[]{:S(2)}, u32[]{:S(2)}) collective-permute-start(f32[2,3,128,128]{3,2,1,0:T(8,128)} %get-tuple-element.57), channel_id=1, source_target_pairs={{0,16},{8,24},{16,0},{24,8},{1,17},{9,25},{17,1},{25,9},{2,18},{10... | collective-permute-start | bytes 1179656 | tf_op jit(solution)/shard_map/ppermute | solution.py:307
  24.5 34.4 %collective-permute-start.11 = (f32[2,3,128,128]{3,2,1,0:T(8,128)}, f32[2,3,128,128]{3,2,1,0:T(8,128)S(1)}, u32[]{:S(2)}, u32[]{:S(2)}) collective-permute-start(f32[2,3,128,128]{3,2,1,0:T(8,128)} %get-tuple-element.58), channel_id=1, source_target_pairs={{0,24},{8,16},{16,8},{24,0},{1,25},{9,17},{17,9},{25,1},{2,26},{10... | collective-permute-start | bytes 1179656 | tf_op jit(solution)/shard_map/ppermute | solution.py:307
  33.5 38.0 %collective-permute-start.1 = (f32[2,2,128,128]{3,2,1,0:T(8,128)}, f32[2,2,128,128]{3,2,1,0:T(8,128)}, u32[]{:S(2)}, u32[]{:S(2)}) collective-permute-start(f32[2,2,128,128]{3,2,1,0:T(8,128)} %get-tuple-element.45), channel_id=1, source_target_pairs={{0,16},{8,24},{16,0},{24,8},{1,17},{9,25},{17,1},{25,9},{2,18},{10... | collective-permute-start | bytes 786440 | tf_op jit(solution)/shard_map/ppermute | solution.py:307
  35.5 36.0 %collective-permute-start.2 = (f32[2,2,128,128]{3,2,1,0:T(8,128)}, f32[2,2,128,128]{3,2,1,0:T(8,128)}, u32[]{:S(2)}, u32[]{:S(2)}) collective-permute-start(f32[2,2,128,128]{3,2,1,0:T(8,128)} %get-tuple-element.46), channel_id=1, source_target_pairs={{0,24},{8,16},{16,8},{24,0},{1,25},{9,17},{17,9},{25,1},{2,26},{10... | collective-permute-start | bytes 786440 | tf_op jit(solution)/shard_map/ppermute | solution.py:307
  41.1 23.5 %collective-permute-start.6 = (f32[2,3,32,128]{3,2,1,0:T(8,128)S(1)}, f32[2,3,32,128]{3,2,1,0:T(8,128)S(1)}, u32[]{:S(2)}, u32[]{:S(2)}) collective-permute-start(f32[2,3,32,128]{3,2,1,0:T(8,128)S(1)} %get-tuple-element.52), channel_id=1, source_target_pairs={{0,2},{1,3},{2,0},{3,1},{4,6},{5,7},{6,4},{7,5},{8,10},{9,11},{10,... | collective-permute-start | bytes 294920 | tf_op jit(solution)/shard_map/ppermute | solution.py:307
  56.0 8.9 %collective-permute-start.7 = (f32[2,3,32,128]{3,2,1,0:T(8,128)S(1)}, f32[2,3,32,128]{3,2,1,0:T(8,128)S(1)}, u32[]{:S(2)}, u32[]{:S(2)}) collective-permute-start(f32[2,3,32,128]{3,2,1,0:T(8,128)S(1)} %get-tuple-element.53), channel_id=1, source_target_pairs={{0,4},{1,5},{2,6},{3,7},{4,0},{5,1},{6,2},{7,3},{8,12},{9,13},{10,... | collective-permute-start | bytes 294920 | tf_op jit(solution)/shard_map/ppermute | solution.py:307
  58.9 8.8 %collective-permute-start.8 = (f32[2,3,32,128]{3,2,1,0:T(8,128)S(1)}, f32[2,3,32,128]{3,2,1,0:T(8,128)S(1)}, u32[]{:S(2)}, u32[]{:S(2)}) collective-permute-start(f32[2,3,32,128]{3,2,1,0:T(8,128)S(1)} %get-tuple-element.54), channel_id=1, source_target_pairs={{0,6},{1,7},{2,4},{3,5},{4,2},{5,3},{6,0},{7,1},{8,14},{9,15},{10,... | collective-permute-start | bytes 294920 | tf_op jit(solution)/shard_map/ppermute | solution.py:307
  64.6 13.7 %collective-permute-start.15 = (f32[2,3,32,128]{3,2,1,0:T(8,128)S(1)}, f32[2,3,32,128]{3,2,1,0:T(8,128)S(1)}, u32[]{:S(2)}, u32[]{:S(2)}) collective-permute-start(f32[2,3,32,128]{3,2,1,0:T(8,128)S(1)} %get-tuple-element.67), channel_id=1, source_target_pairs={{0,2},{1,3},{2,0},{3,1},{4,6},{5,7},{6,4},{7,5},{8,10},{9,11},{10,... | collective-permute-start | bytes 294920 | tf_op jit(solution)/shard_map/ppermute | solution.py:307
  64.9 15.7 %collective-permute-start.16 = (f32[2,3,32,128]{3,2,1,0:T(8,128)S(1)}, f32[2,3,32,128]{3,2,1,0:T(8,128)S(1)}, u32[]{:S(2)}, u32[]{:S(2)}) collective-permute-start(f32[2,3,32,128]{3,2,1,0:T(8,128)S(1)} %get-tuple-element.68), channel_id=1, source_target_pairs={{0,4},{1,5},{2,6},{3,7},{4,0},{5,1},{6,2},{7,3},{8,12},{9,13},{10,... | collective-permute-start | bytes 294920 | tf_op jit(solution)/shard_map/ppermute | solution.py:307
  67.7 12.9 %collective-permute-start.17 = (f32[2,3,32,128]{3,2,1,0:T(8,128)S(1)}, f32[2,3,32,128]{3,2,1,0:T(8,128)S(1)}, u32[]{:S(2)}, u32[]{:S(2)}) collective-permute-start(f32[2,3,32,128]{3,2,1,0:T(8,128)S(1)} %get-tuple-element.69), channel_id=1, source_target_pairs={{0,6},{1,7},{2,4},{3,5},{4,2},{5,3},{6,0},{7,1},{8,14},{9,15},{10,... | collective-permute-start | bytes 294920 | tf_op jit(solution)/shard_map/ppermute | solution.py:307
  71.5 1.0 copy-start.1
  76.1 6.1 %collective-permute-start.12 = (f32[2,2,32,128]{3,2,1,0:T(8,128)S(1)}, f32[2,2,32,128]{3,2,1,0:T(8,128)S(1)}, u32[]{:S(2)}, u32[]{:S(2)}) collective-permute-start(f32[2,2,32,128]{3,2,1,0:T(8,128)S(1)} %get-tuple-element.63), channel_id=1, source_target_pairs={{0,2},{1,3},{2,0},{3,1},{4,6},{5,7},{6,4},{7,5},{8,10},{9,11},{10,... | collective-permute-start | bytes 196616 | tf_op jit(solution)/shard_map/ppermute | solution.py:307
  77.9 5.6 %collective-permute-start.13 = (f32[2,2,32,128]{3,2,1,0:T(8,128)S(1)}, f32[2,2,32,128]{3,2,1,0:T(8,128)S(1)}, u32[]{:S(2)}, u32[]{:S(2)}) collective-permute-start(f32[2,2,32,128]{3,2,1,0:T(8,128)S(1)} %get-tuple-element.64), channel_id=1, source_target_pairs={{0,4},{1,5},{2,6},{3,7},{4,0},{5,1},{6,2},{7,3},{8,12},{9,13},{10,... | collective-permute-start | bytes 196616 | tf_op jit(solution)/shard_map/ppermute | solution.py:307
  78.3 6.2 %collective-permute-start.14 = (f32[2,2,32,128]{3,2,1,0:T(8,128)S(1)}, f32[2,2,32,128]{3,2,1,0:T(8,128)S(1)}, u32[]{:S(2)}, u32[]{:S(2)}) collective-permute-start(f32[2,2,32,128]{3,2,1,0:T(8,128)S(1)} %get-tuple-element.65), channel_id=1, source_target_pairs={{0,6},{1,7},{2,4},{3,5},{4,2},{5,3},{6,0},{7,1},{8,14},{9,15},{10,... | collective-permute-start | bytes 196616 | tf_op jit(solution)/shard_map/ppermute | solution.py:307
where the time goes:
time: 99.2 us; the launch traced here: 99 us
  starting transfers between devices  28.8 us (29%)
  waiting for transfers between devices  28.5 us (29%)
  Pallas kernels  27 us (27%)
  blocking collectives  11.1 us (11%)
  local copies, waits for them, and re-layouts  1.92 us (2%)
    ppermute x18, starting transfers between devices, swap_with(): lax.ppermute(x, axis, [(i, i ^ mask) for i in range(lax.axis_size(axis))])  28.8 us
    ppermute x18, waiting for transfers between devices, swap_with(): lax.ppermute(x, axis, [(i, i ^ mask) for i in range(lax.axis_size(axis))])  28.5 us
    pallas_call x3, Pallas kernels, first(): pl.pallas_call(functools.partial(first_kernel, fresh), in_specs=[smem] *...  12.1 us
    all_to_all x1, blocking collectives, shards(): gathered = lax.all_to_all(sums, ('gx', 'gy'), 0, 0)  11.1 us
    pallas_call x3, Pallas kernels, encode(): pl.pallas_call(functools.partial(encode_kernel, starts[c]), in_specs=[sme...  9.3 us
    pallas_call x3, Pallas kernels, second(): pl.pallas_call(functools.partial(second_kernel, starts[c], fresh, last),...  5.53 us
  transfers between devices with their start and end apart: 18, of which 5 were waited for; matrix products, arithmetic and copies ran while one was open for 0% of the time, Pallas kernels for 22%

commit v1 on v0

v1 whole, which is shorter than its diff:
```python
import functools

import jax
import jax.numpy as jnp
from jax import lax
from jax.experimental import pallas as pl
from jax.experimental.pallas import tpu as pltpu
from jax.sharding import PartitionSpec as P


PRIME = 2147483647
LANES = 128
UNROLL = 4
VMEM_ENCODE, VMEM_KERNEL = 16 << 20, 8 << 20


def shr(x, n):
    return lax.shift_right_logical(x, jnp.int32(n))


def reduce_once(x):
    return (x & PRIME) + shr(x, 31)


def add_mod(a, b):
    return reduce_once(a + b)


def sub_mod(a, b):
    return reduce_once(a + (PRIME - b))


def limbs_of(v):
    return v & 2047, shr(v, 11) & 2047, shr(v, 22)


def word_of_limbs(l0, l1, l2):
    half = jnp.floor(l2 * 0.5)
    base = (l0 + l1 * 2048.0) + ((l2 - half * 2.0) * 4194304.0 + 8388608.0)
    negative = half >= 128.0
    scale = jnp.exp2(half - jnp.where(negative, 192.0, 64.0))
    return base * jnp.where(negative, -scale, scale)


def word_of_int(v):
    base = ((v & 8388607) + 8388608).astype(jnp.float32)
    negative = v >= 1073741824
    scale = jnp.exp2(((shr(v, 23) & 127) - 64).astype(jnp.float32))
    return base * jnp.where(negative, -scale, scale)


def int_of_word(x):
    size = jnp.abs(x)
    level = jnp.floor(jnp.log2(size) + 0.0009765625)
    value = size * jnp.exp2(23.0 - level)
    value = jnp.minimum(value, value + value - 8388608.0)
    offset = jnp.where(x < 0.0, jnp.int32((40 << 23) + (1 << 30)), jnp.int32(40 << 23))
    return value.astype(jnp.int32) + (level.astype(jnp.int32) << 23) + offset


def weighted_sum(limbs, weights):
    low = high = None
    for a, c in zip(limbs, weights):
        for n in range(3):
            low = a[n] * c[n] if low is None else low + a[n] * c[n]
            high = a[n] * c[3 + n] if high is None else high + a[n] * c[3 + n]
    return reduce_once(low + ((high & 32767) << 16) + shr(high, 15))


def degrees(a, b):
    return [
        a[0] * b[0],
        a[0] * b[1] + a[1] * b[0],
        a[0] * b[2] + a[1] * b[1] + a[2] * b[0],
        a[1] * b[2] + a[2] * b[1],
        a[2] * b[2],
    ]


def rotate(x, n):
    return ((x << n) & PRIME) + shr(x, 31 - n)


def element_of_degrees(d):
    total = add_mod(reduce_once(d[0]), rotate(d[1], 11))
    total = add_mod(total, rotate(d[2], 22))
    total = add_mod(total, rotate(d[3], 2))
    return add_mod(total, rotate(d[4], 13))


def mul_mod(a, b):
    return element_of_degrees(degrees(limbs_of(a), limbs_of(b)))


def add_limbs(a, b):
    return [x + y for x, y in zip(a, b)]


def nine_of(v):
    s02, s13 = add_limbs(v[0], v[2]), add_limbs(v[1], v[3])
    s01, s23 = add_limbs(v[0], v[1]), add_limbs(v[2], v[3])
    return [*v, s02, s13, s01, s23, add_limbs(s01, s23)]


MANY, ALL = range(8), range(9)


def clear(acc_ref, kinds):
    for kind in kinds:
        for n in range(5):
            acc_ref[5 * kind + n] = jnp.zeros((8, LANES), jnp.int32)


def two_rounds(acc_ref, splat_ref, s, w):
    s, w = [[x if isinstance(x, tuple) else limbs_of(x) for x in v] for v in (s, w)]
    for kind, (a, b) in enumerate(zip(nine_of(s), nine_of(w))):
        for n, d in enumerate(degrees(a, b)):
            acc_ref[5 * kind + n] = acc_ref[5 * kind + n] + d
    weights = [[splat_ref[6 * x + n] for n in range(6)] for x in range(4)]
    return weighted_sum(s, weights), weighted_sum(w, weights)


def flush(acc_ref, points_ref, first, kinds):
    for kind in kinds:
        here = element_of_degrees([acc_ref[5 * kind + n] for n in range(5)])
        points_ref[first + kind] = add_mod(points_ref[first + kind], here)


def over_pairs(count, tiles, accs, pair):
    assert tiles <= 16
    rare = [MANY if count * tiles <= 64 else () for _ in accs]

    def body(j, _):
        for (acc_ref, _, _), late in zip(accs, rare):
            clear(acc_ref, [k for k in ALL if k not in late])
        pair(j)
        for (acc_ref, points_ref, first), late in zip(accs, rare):
            flush(acc_ref, points_ref, first, [k for k in ALL if k not in late])

    for (acc_ref, _, _), late in zip(accs, rare):
        clear(acc_ref, late)
    lax.fori_loop(0, count, body, None)
    for (acc_ref, points_ref, first), late in zip(accs, rare):
        flush(acc_ref, points_ref, first, late)


def whole(scalar):
    return jnp.full((8, LANES), scalar, jnp.int32)


def sides(challenges_ref, place, phase):
    out = []
    for k in range(2):
        high = whole(challenges_ref[2 * phase + k])
        low = jnp.where(high == 0, 1, PRIME - high + 1)
        is_low = whole((place >> (1 - k)) & 1) == 0
        out.append((jnp.where(is_low, low, high), jnp.where(is_low, high, low)))
    return out


def constants_of(weight):
    parts = [weight, rotate(weight, 11), rotate(weight, 22)]
    return [x & 65535 for x in parts] + [shr(x, 16) for x in parts]


def splat_weights(challenges_ref, place, phase, splat_ref):
    first, second = sides(challenges_ref, place, phase)
    for x in range(4):
        for n, c in enumerate(constants_of(mul_mod(first[x >> 1], second[x & 1]))):
            splat_ref[6 * x + n] = c


def tile(start, i):
    return pl.ds(pl.multiple_of(start + i * 8, 8), 8)


def start_owns(owns, place, tables, outs, sems):
    copies = []
    for n, (start, count) in enumerate(owns):
        for t in range(2):
            out = outs[2 * n + t]
            rows = out.shape[2]
            src = tables[t].at[:, pl.ds(start, count), pl.ds(pl.multiple_of(place * rows, rows), rows), :]
            copies.append(pltpu.make_async_copy(src, out, sems.at[n, t]))
    for copy in copies:
        copy.start()
    return copies


def encode_kernel(raw, start, owns, gx_ref, gy_ref, s_hbm, w_hbm, *refs):
    if len(owns):
        refs, own_sems = refs[:-1], refs[-1]
    buffer, sems = refs[-2:]
    refs = refs[:-2]
    if len(owns):
        refs, own_outs = refs[: -2 * len(owns)], refs[-2 * len(owns) :]
    token_ref = refs[-1]
    outs = refs[-5:-1] if raw else refs[-4:-1]
    count, rows = buffer.shape[0], buffer.shape[4]
    shifts = (1, 2, 3, 0) if raw else (1, 2, 3)
    order = [(j, d, t) for j in range(count) for d in shifts for t in range(2)]

    def copy(j, d, t):
        src = (s_hbm, w_hbm)[t].at[:, start + j, pl.ds(pl.multiple_of((gx_ref[0] ^ d) * rows, rows), rows), :]
        return pltpu.make_async_copy(src, buffer.at[j, d % len(shifts), t], sems.at[j, d % len(shifts), t])

    for where in order:
        copy(*where).start()
    if len(owns):
        own_copies = start_owns(owns, gx_ref[0], (s_hbm, w_hbm), own_outs, own_sems)
    token_ref[...] = jnp.zeros_like(token_ref)
    sub = rows // 4
    for where in order:
        j, d, t = where
        slot = d % len(shifts)
        copy(*where).wait()
        for e in range(4 if raw else 1):
            first = (gy_ref[0] ^ e) * sub if raw else 0

            def step(i, _):
                word = word_of_limbs(*[buffer[j, slot, t, n, tile(first, i)] for n in range(3)])
                if raw:
                    outs[e][t, j, d, tile(0, i)] = word
                else:
                    outs[d - 1][t, j, tile(0, i)] = word

            lax.fori_loop(0, (sub if raw else rows) // 8, step, None, unroll=4)
    if len(owns):
        for copy_own in own_copies:
            copy_own.wait()


def gather_kernel(z0, z1, z2, z3, o1, o2, o3):
    for e, src in enumerate((z0, z1, z2, z3)):
        for d, out in enumerate((o1, o2, o3)):
            for t in range(2):
                for j in range(out.shape[1]):
                    out[t, j, e] = src[t, j, d + 1]


def first_kernel(fresh, challenges_ref, gx_ref, gy_ref, s_ref, w_ref, g1, g2, g3, *refs):
    if not fresh:
        before_ref, *refs = refs
    points_ref, kept_ref, o1, o2, o3, acc_ref, splat_ref = refs
    count, rows = s_ref.shape[1], s_ref.shape[2]
    sub = rows // 4
    given, outs = (g1, g2, g3), (kept_ref, o1, o2, o3)
    splat_weights(challenges_ref, gx_ref[0], 0, splat_ref)
    points_ref[...] = jnp.zeros_like(points_ref) if fresh else before_ref[...]

    def pair(j):
        for e in range(4):
            start = (gy_ref[0] ^ e) * sub

            def step(i, _):
                at = tile(start, i)
                values = []
                for t, own in enumerate((s_ref, w_ref)):
                    limbs = tuple(own[n, j, at].astype(jnp.int32) for n in range(3))
                    values.append([limbs] + [int_of_word(g[t, j, at]) for g in given])
                for t, folded in enumerate(two_rounds(acc_ref, splat_ref, *values)):
                    outs[e][t, j, tile(0, i)] = word_of_int(folded) if e else folded

            lax.fori_loop(0, sub // 8, step, None, unroll=UNROLL)

    over_pairs(count, rows // 8, [(acc_ref, points_ref, 0)], pair)


def settle(lowest, middle, highest, passes=3):
    for _ in range(passes):
        carried = jnp.floor(lowest * (1.0 / 2048.0))
        lowest = lowest - carried * 2048.0
        middle = middle + carried
        carried = jnp.floor(middle * (1.0 / 2048.0))
        middle = middle - carried * 2048.0
        highest = highest + carried
        carried = jnp.floor(highest * (1.0 / 512.0))
        highest = highest - carried * 512.0
        lowest = lowest + carried
    if passes < 3:
        return lowest, middle, highest
    at_modulus = (lowest == 2047.0) & (middle == 2047.0) & (highest == 511.0)
    return [jnp.where(at_modulus, 0.0, limb) for limb in (lowest, middle, highest)]


def round_sums(challenges_ref, place, phase, points):
    own, other = sides(challenges_ref, place, phase)[0]
    squares = [constants_of(mul_mod(*x)) for x in ((own, own), (own, other), (other, other))]
    i0, i1, i2, i3, i02, i13, i01, i23, i0123 = points
    first = [add_mod(i0, i1), add_mod(i2, i3), add_mod(i02, i13)]
    second = []
    for own, other, both in ((i0, i2, i02), (i1, i3, i13), (i01, i23, i0123)):
        cross = sub_mod(both, add_mod(own, other))
        second.append(weighted_sum([limbs_of(x) for x in (own, cross, other)], squares))
    return [first, second]


def publish_row(challenges_ref, places, points_ref, sums_ref):
    lane = lax.broadcasted_iota(jnp.int32, (1, LANES), 1)
    rows = [jnp.zeros((1, LANES), jnp.float32) for _ in range(3)]
    for phase in range(2):
        place = places[phase]
        points = [points_ref[9 * phase + n] for n in range(9)]
        for k, (own, other, both) in enumerate(round_sums(challenges_ref, place, phase, points)):
            is_low = whole((place >> (1 - k)) & 1) == 0
            at_zero = jnp.where(is_low, own, other)
            at_one = jnp.where(is_low, other, own)
            once = add_mod(at_zero, add_mod(at_one, at_one))
            at_two = sub_mod(add_mod(once, add_mod(once, once)), add_mod(both, both))
            for t, value in enumerate((at_zero, at_one, at_two)):
                for n, limb in enumerate(limbs_of(value)):
                    total = jnp.sum(limb.astype(jnp.float32), axis=(0, 1), keepdims=True)
                    rows[n] = jnp.where(lane == 6 * phase + 3 * k + t, total, rows[n])
    low, mid, high = settle(*rows, passes=1)
    packed = low + pltpu.roll(mid, 16, 1) + pltpu.roll(high, 32, 1)
    sums_ref[...] = jnp.broadcast_to(packed, sums_ref.shape)


class Finish:
    def __init__(self, early, late, s_ref, w_ref, refs):
        self.sums_ref, s_hbm, w_hbm, sems = refs
        self.parts = [
            [
                pltpu.make_async_copy(src.at[:, part], dst.at[:, part], sems.at[which, t])
                for t, (src, dst) in enumerate(((s_ref, s_hbm), (w_ref, w_hbm)))
            ]
            for which, part in enumerate((pl.ds(*early), pl.ds(*late)))
        ]
        self.start(0)

    def start(self, which):
        for copy in self.parts[which]:
            copy.start()

    def end(self, challenges_ref, places, points_ref):
        self.start(1)
        publish_row(challenges_ref, places, points_ref, self.sums_ref)
        for copy in self.parts[0] + self.parts[1]:
            copy.wait()


def put_folded(outs, j, at, folded):
    for out, value in zip(outs, folded):
        for n, limb in enumerate(limbs_of(jnp.where(value == PRIME, 0, value))):
            out[n, j, at] = limb.astype(jnp.float32)


def second_kernel(start, fresh, last, challenges_ref, gx_ref, gy_ref, kept_ref, g1, g2, g3, before_ref, *refs):
    if not fresh:
        refs = refs[2:]
    points_ref, s_ref, w_ref, *refs = refs
    count, rows = kept_ref.shape[1], kept_ref.shape[2]
    if last:
        finish = Finish((0, start), (start, count), s_ref, w_ref, refs[:3] + refs[5:])
        refs = refs[3:5]
    acc_ref, splat_ref = refs
    given = (g1, g2, g3)
    splat_weights(challenges_ref, gy_ref[0], 1, splat_ref)
    points_ref[...] = before_ref[...]

    def pair(j):
        def step(i, _):
            at = tile(0, i)
            s, w = [[kept_ref[t, j, at]] + [int_of_word(g[t, j, at]) for g in given] for t in range(2)]
            put_folded((s_ref, w_ref), start + j, at, two_rounds(acc_ref, splat_ref, s, w))

        lax.fori_loop(0, rows // 8, step, None, unroll=UNROLL)

    over_pairs(count, rows // 8, [(acc_ref, points_ref, 9)], pair)
    if last:
        finish.end(challenges_ref, (gx_ref[0], gy_ref[0]), points_ref)


def all_kernel(start, fresh, last, challenges_ref, gx_ref, gy_ref, z0, z1, z2, z3, g1, g2, g3, before_ref, *refs):
    if not fresh:
        refs = refs[2:]
    points_ref, s_ref, w_ref, *refs = refs
    count, rows = z0.shape[1], z0.shape[3]
    if last:
        finish = Finish((0, start), (start, count), s_ref, w_ref, refs[:3] + refs[5 + 3 :])
        refs = refs[3 : 5 + 3]
    acc_ref, splat_ref, acc2_ref, splat2_ref, once = refs
    given = (g1, g2, g3)
    splat_weights(challenges_ref, gx_ref[0], 0, splat_ref)
    splat_weights(challenges_ref, gy_ref[0], 1, splat2_ref)
    points_ref[...] = before_ref[...]

    def pair(j):
        for e, own in enumerate((z0, z1, z2, z3)):

            def step(i, _):
                at = tile(0, i)
                s, w = [[int_of_word(x) for x in [own[t, j, 0, at]] + [g[t, j, e, at] for g in given]] for t in range(2)]
                for t, folded in enumerate(two_rounds(acc_ref, splat_ref, s, w)):
                    once[t, e, at] = folded

            lax.fori_loop(0, rows // 8, step, None, unroll=UNROLL)

        def step(i, _):
            at = tile(0, i)
            s, w = [[once[t, e, at] for e in range(4)] for t in range(2)]
            put_folded((s_ref, w_ref), start + j, at, two_rounds(acc2_ref, splat2_ref, s, w))

        lax.fori_loop(0, rows // 8, step, None, unroll=UNROLL)

    over_pairs(count, rows // 2, [(acc_ref, points_ref, 0), (acc2_ref, points_ref, 9)], pair)
    if last:
        finish.end(challenges_ref, (gx_ref[0], gy_ref[0]), points_ref)


def swap_with(x, axis, mask):
    return lax.ppermute(x, axis, [(i, i ^ mask) for i in range(lax.axis_size(axis))])


CHUNKS, RAW = (3, 3), 2
SENDS = "0R1"
STEPS = ("A0", "G", "A1", "B0", "K", "B1")
POINTS = pltpu.VMEM((18, 8, LANES), jnp.int32)


def plan(polynomials):
    if sum(CHUNKS) + RAW == polynomials:
        return CHUNKS, RAW, SENDS, STEPS
    sizes = (1,) * polynomials
    steps = ["A0"] + [x for c in range(1, polynomials) for x in (f"A{c}", f"B{c - 1}")] + [f"B{polynomials - 1}"]
    return sizes, 0, range(polynomials), steps


def shards(devices, selectors, proofs, challenges):
    polynomials, row_count = selectors.shape[1], selectors.shape[-1]
    lane_rows = row_count // LANES
    quarter, final = lane_rows // 4, lane_rows // 16
    tables = [
        pltpu.with_memory_space_constraint(x.reshape(3, polynomials, lane_rows, LANES), pltpu.HBM)
        for x in (selectors, proofs)
    ]
    gx_shift = lax.axis_size("gx").bit_length() - 3
    gy_shift = lax.axis_size("gy").bit_length() - 3
    gx_place = (lax.axis_index("gx") >> gx_shift).astype(jnp.int32).reshape(1)
    gy_place = (lax.axis_index("gy") >> gy_shift).astype(jnp.int32).reshape(1)

    sizes, raw, sends, steps = plan(polynomials)
    raw_last = steps[-1] == "K"
    raw_start = polynomials - raw if raw_last else 0
    starts = [sum(sizes[:c]) + (0 if raw_last else raw) for c in range(len(sizes))]
    smem, vmem, hbm, anywhere = [pl.BlockSpec(memory_space=m) for m in (pltpu.SMEM, pltpu.VMEM, pltpu.HBM, pl.ANY)]

    def words(count, rows, dtype=jnp.float32):
        return pltpu.VMEM((2, count, *rows, LANES), dtype)

    def near(arrays):
        return [pltpu.with_memory_space_constraint(x, pltpu.VMEM) for x in arrays]

    work = [pltpu.VMEM((45, 8, LANES), jnp.int32), pltpu.VMEM((24, 8, LANES), jnp.int32)]
    small = pltpu.CompilerParams(vmem_limit_bytes=VMEM_KERNEL)

    def encode(raw_chunk, start, count, outs, owns, token):
        out_shape = outs + [pltpu.VMEM((8, LANES), jnp.float32)]
        out_shape += [pltpu.VMEM((3, n, quarter, LANES), jnp.float32) for _, n in owns for _ in range(2)]
        shifts = 4 if raw_chunk else 3
        scratch = [
            pltpu.VMEM((count, shifts, 2, 3, quarter, LANES), jnp.float32),
            pltpu.SemaphoreType.DMA((count, shifts, 2)),
        ]
        if owns:
            scratch.append(pltpu.SemaphoreType.DMA((len(owns), 2)))
        return pl.pallas_call(
            functools.partial(encode_kernel, raw_chunk, start, owns),
            in_specs=[smem, smem, hbm, hbm] + [anywhere] * len(token),
            out_specs=[vmem] * len(out_shape),
            out_shape=out_shape,
            scratch_shapes=scratch,
            compiler_params=pltpu.CompilerParams(vmem_limit_bytes=VMEM_ENCODE),
            name="encode",
        )(gx_place, gy_place, *tables, *token)

    def first(c, own, given, before):
        count = sizes[c]
        fresh = before is None
        return pl.pallas_call(
            functools.partial(first_kernel, fresh),
            in_specs=[smem] * 3 + [vmem] * (5 if fresh else 6),
            out_specs=[vmem] * 5,
            out_shape=[POINTS, words(count, [final], jnp.int32)] + [words(count, [final])] * 3,
            scratch_shapes=work,
            input_output_aliases={} if fresh else {8: 0},
            compiler_params=small,
            name="first_rounds",
        )(challenges, gx_place, gy_place, *own, *near(given), *(() if fresh else (before,)))

    def fold_last(kernel, start, arrays, before, folded, last, scratch):
        fresh = folded is None
        shape = (3, polynomials, final, LANES)
        out_shape, out_specs = [POINTS] + [pltpu.VMEM(shape, jnp.float32)] * 2, [vmem] * 3
        if last:
            out_shape += [jax.ShapeDtypeStruct((devices, 1, LANES), jnp.float32)] + [jax.ShapeDtypeStruct(shape, jnp.float32)] * 2
            out_specs += [vmem, hbm, hbm]
            scratch = scratch + [pltpu.SemaphoreType.DMA((2, 2))]
        at = 3 + len(arrays)
        return pl.pallas_call(
            functools.partial(kernel, start, fresh, last),
            in_specs=[smem] * 3 + [vmem] * (len(arrays) + (1 if fresh else 3)),
            out_specs=out_specs,
            out_shape=out_shape,
            scratch_shapes=scratch,
            input_output_aliases={at: 0} if fresh else {at: 0, at + 1: 1, at + 2: 2},
            compiler_params=small,
        )(challenges, gx_place, gy_place, *near(arrays), before, *(() if fresh else folded))

    def swap(arrays, axis, shift):
        return [swap_with(x, axis, (d + 1) << shift) for d, x in enumerate(arrays)]

    owns, sent, token = {}, {}, []
    reader = list(sends)[min(1, len(sends) - 1)]
    ranges = list(zip(starts, sizes))
    for c in sends:
        raw_chunk = c == "R"
        if raw_chunk:
            start, count, outs = raw_start, raw, [words(raw, [4, final])] * 4
        else:
            start, count = ranges[int(c)]
            outs = [words(count, [quarter])] * 3
        out = encode(raw_chunk, start, count, outs, ranges if c == reader else [], token)
        given, token = out[: len(outs)], [out[len(outs)]]
        if raw_chunk:
            raw_own, *given = given
        if c == reader:
            rest = out[len(outs) + 1 :]
            owns = {n: rest[2 * n : 2 * n + 2] for n in range(len(ranges))}
        sent[c if raw_chunk else int(c)] = swap(given, *(("gy", gy_shift) if raw_chunk else ("gx", gx_shift)))
    points, folded, waiting = None, None, {}
    for step in steps:
        last = step == steps[-1]
        c = int(step[1:] or 0)
        if step[0] == "A":
            points, kept, *given = first(c, owns[c], sent[c], points)
        elif step[0] == "G":
            around = [raw_own, *sent["R"]]
            given = pl.pallas_call(
                gather_kernel,
                in_specs=[vmem] * 4,
                out_specs=[vmem] * 3,
                out_shape=[words(raw, [4, final])] * 3,
                compiler_params=small,
                name="gather",
            )(*near(around))
        elif step[0] == "K":
            scratch = work + work + [pltpu.VMEM((2, 4, final, LANES), jnp.int32)]
            points, *folded = fold_last(all_kernel, raw_start, around + given_raw, points, folded, last, scratch)
        else:
            points, *folded = fold_last(second_kernel, starts[c], waiting[c], points, folded, last, work)
        if step[0] == "A":
            waiting[c] = [kept, *swap(given, "gy", gy_shift)]
        elif step[0] == "G":
            given_raw = swap(given, "gx", gx_shift)
    sums, *folded = folded[2:]
    gathered = lax.all_to_all(sums, ("gx", "gy"), 0, 0)
    total = gathered.sum(axis=0).reshape(LANES)
    points = jnp.stack(settle(total[0:12], total[16:28], total[32:44])).reshape(3, 4, 3)
    shape = (3, polynomials, 1, 1, row_count // 16)
    return points, folded[0].reshape(shape), folded[1].reshape(shape)


def solution(mesh):
    tables = P(None, None, "gx", "gy", None)
    devices = mesh.shape["gx"] * mesh.shape["gy"]

    def body(*arrays):
        return shards(devices, *arrays)

    return jax.shard_map(
        body,
        mesh=mesh,
        in_specs=(tables, tables, P()),
        out_specs=(P(), tables, tables),
        check_vma=False,
    )
```

time: 99.2 us -> 91.5 us (0.922)
  starting transfers between devices: 28.8 us -> 23.3 us
  waiting for transfers between devices: 28.5 us -> 33.2 us
  Pallas kernels: 27 us -> 22.8 us
  local copies, waits for them, and re-layouts: 1.92 us -> 0.25 us
  blocking collectives: 11.1 us -> 10.1 us
    ppermute x18, starting transfers between devices: 28.8 us -> 23.3 us  [swap_with(): lax.ppermute(x, axis, [(i, i ^ mask) for i in range(lax.axis_size(axis))])]
    ppermute x18, waiting for transfers between devices: 28.5 us -> 33.2 us  [swap_with(): lax.ppermute(x, axis, [(i, i ^ mask) for i in range(lax.axis_size(axis))])]
    pallas_call x3 -> x2, Pallas kernels: 12.1 us -> 7.43 us  [first(): pl.pallas_call(functools.partial(first_kernel, fresh), in_specs=[smem] *...]
    unnamed x6 -> x2, local copies, waits for them, and re-layouts: 1.67 us -> 0.01 us
    pallas_call x6 -> x7, Pallas kernels: 14.8 us -> 15.4 us  [the longest x3 8.19 us: encode(): pl.pallas_call(functools.partial(encode_kernel, raw_chunk, start, owns),...]
  transfers between devices with their start and end apart: 18 -> 18, of which waited for: 5 -> 7; matrix products, arithmetic and copies ran while one was open for 0% -> 0% of each run, Pallas kernels for 22% -> 20%
where the time goes in v1:
time: 91.5 us; the launch traced here: 91.3 us
  waiting for transfers between devices  33.2 us (36%)
  starting transfers between devices  23.3 us (25%)
  Pallas kernels  22.8 us (25%)
  blocking collectives  10.1 us (11%)
    ppermute x18, waiting for transfers between devices, swap_with(): lax.ppermute(x, axis, [(i, i ^ mask) for i in range(lax.axis_size(axis))])  33.2 us
    ppermute x18, starting transfers between devices, swap_with(): lax.ppermute(x, axis, [(i, i ^ mask) for i in range(lax.axis_size(axis))])  23.3 us
    all_to_all x1, blocking collectives, shards(): gathered = lax.all_to_all(sums, ('gx', 'gy'), 0, 0)  10.1 us
    pallas_call x3, Pallas kernels, encode(): pl.pallas_call(functools.partial(encode_kernel, raw_chunk, start, owns),...  8.19 us
    pallas_call x2, Pallas kernels, first(): pl.pallas_call(functools.partial(first_kernel, fresh), in_specs=[smem] *...  7.43 us
    pallas_call x3, Pallas kernels, fold_last(): pl.pallas_call(functools.partial(kernel, start, fresh, last), in_specs=[s...  7.14 us
  transfers between devices with their start and end apart: 18, of which 7 were waited for; matrix products, arithmetic and copies ran while one was open for 0% of the time, Pallas kernels for 20%

profile of v1, /device:TPU:0, one launch (start us, length us, event | category | flops | bytes accessed | tf_op | source)
XLA Modules:
  0.0 91.3 jit_solution(6466172223684803035)
XLA Ops:
  0.6 2.4 %encode.3 = (f32[2,3,128,128]{3,2,1,0:T(8,128)S(1)}, f32[2,3,128,128]{3,2,1,0:T(8,128)S(1)}, f32[2,3,128,128]{3,2,1,0:T(8,128)S(1)}, f32[8,128]{1,0:T(8,128)S(1)}) custom-call(s32[1]{0:T(128)} %bitcast.gx_ref, s32[1]{0:T(128)} %bitcast.1.gy_ref, f32[3,8,512,128]{3,2,1,0:T(8,128)} %bitcast.7, f32[3,8,512,128]{3,2,1,0:T(8,128)} %bitcast.10), custom_call_target="tpu_custom_call" | custom-call | tf_op jit(solution)/shard_map/encode/pallas_call | solution.py:467
  3.0 3.0 %collective-permute-start.3 = (f32[2,3,128,128]{3,2,1,0:T(8,128)S(1)}, f32[2,3,128,128]{3,2,1,0:T(8,128)S(1)}, u32[]{:S(2)}, u32[]{:S(2)}) collective-permute-start(f32[2,3,128,128]{3,2,1,0:T(8,128)S(1)} %get-tuple-element.50), channel_id=1, source_target_pairs={{0,8},{8,0},{16,24},{24,16},{1,9},{9,1},{17,25},{25,17},{2,10},{10... | collective-permute-start | bytes 1179656 | tf_op jit(solution)/shard_map/ppermute | solution.py:412
  6.1 2.8 %encode.4 = (f32[2,2,4,32,128]{4,3,2,1,0:T(8,128)S(1)}, f32[2,2,4,32,128]{4,3,2,1,0:T(8,128)S(1)}, f32[2,2,4,32,128]{4,3,2,1,0:T(8,128)S(1)}, f32[2,2,4,32,128]{...) custom-call(s32[1]{0:T(128)} %bitcast.gx_ref, ...), custom_call_target="tpu_custom_call" | custom-call | tf_op jit(solution)/shard_map/encode/pallas_call | solution.py:467
  8.9 2.7 %collective-permute-start.10 = (f32[2,2,4,32,128]{4,3,2,1,0:T(8,128)S(1)}, f32[2,2,4,32,128]{4,3,2,1,0:T(8,128)S(1)}, u32[]{:S(2)}, u32[]{:S(2)}) collective-permute-start(f32[2,2,4,32,128]{4,3,2,1,0:T(8,128)S(1)} %get-tuple-element.60), channel_id=1, source_target_pairs={{0,4},{1,5},{2,6},{3,7},{4,0},{5,1},{6,2},{7,3},{8,12},{9,13},{10,... | collective-permute-start | bytes 786440 | tf_op jit(solution)/shard_map/ppermute | solution.py:412
  11.6 1.3 %collective-permute-start.11 = (f32[2,2,4,32,128]{4,3,2,1,0:T(8,128)S(1)}, f32[2,2,4,32,128]{4,3,2,1,0:T(8,128)S(1)}, u32[]{:S(2)}, u32[]{:S(2)}) collective-permute-start(f32[2,2,4,32,128]{4,3,2,1,0:T(8,128)S(1)} %get-tuple-element.61), channel_id=1, source_target_pairs={{0,6},{1,7},{2,4},{3,5},{4,2},{5,3},{6,0},{7,1},{8,14},{9,15},{10,... | collective-permute-start | bytes 786440 | tf_op jit(solution)/shard_map/ppermute | solution.py:412
  12.9 0.2 collective-permute-start.9
  13.1 1.5 %collective-permute-start.4 = (f32[2,3,128,128]{3,2,1,0:T(8,128)S(1)}, f32[2,3,128,128]{3,2,1,0:T(8,128)S(1)}, u32[]{:S(2)}, u32[]{:S(2)}) collective-permute-start(f32[2,3,128,128]{3,2,1,0:T(8,128)S(1)} %get-tuple-element.51), channel_id=1, source_target_pairs={{0,16},{8,24},{16,0},{24,8},{1,17},{9,25},{17,1},{25,9},{2,18},{10... | collective-permute-start | bytes 1179656 | tf_op jit(solution)/shard_map/ppermute | solution.py:412
  14.7 15.4 %collective-permute-done.10.z2 = f32[2,2,4,32,128]{4,3,2,1,0:T(8,128)S(1)} collective-permute-done((f32[2,2,4,32,128]{4,3,2,1,0:T(8,128)S(1)}, f32[2,2,4,32,128]{4,3,2,1,0:T(8,128)S(1)}, u32[]{:S(2)}, u32[]{:S(2)}) %collective-permute-start.10) | collective-permute-done | bytes 262176 | tf_op jit(solution)/shard_map/ppermute | solution.py:412
  30.0 1.5 %collective-permute-start.5 = (f32[2,3,128,128]{3,2,1,0:T(8,128)S(1)}, f32[2,3,128,128]{3,2,1,0:T(8,128)S(1)}, u32[]{:S(2)}, u32[]{:S(2)}) collective-permute-start(f32[2,3,128,128]{3,2,1,0:T(8,128)S(1)} %get-tuple-element.52), channel_id=1, source_target_pairs={{0,24},{8,16},{16,8},{24,0},{1,25},{9,17},{17,9},{25,1},{2,26},{10... | collective-permute-start | bytes 1179656 | tf_op jit(solution)/shard_map/ppermute | solution.py:412
  31.5 3.0 %encode.5 = (f32[2,3,128,128]{3,2,1,0:T(8,128)S(1)}, f32[2,3,128,128]{3,2,1,0:T(8,128)S(1)}, f32[2,3,128,128]{3,2,1,0:T(8,128)S(1)}, f32[8,128]{1,0:T(8,128)}) custom-call(s32[1]{0:T(128)} %bitcast.gx_ref, s32[1]{0:T(128)} %bitcast.1.gy_ref, f32[3,8,512,128]{3,2,1,0:T(8,128)} %bitcast.9, f32[3,8,512,128]{3,2,1,0:T(8,128)} %bitcast.12, ...), custom_call_target="tpu_custom_call" | custom-call | tf_op jit(solution)/shard_map/encode/pallas_call | solution.py:467
  34.5 1.6 %collective-permute-start = (f32[2,3,128,128]{3,2,1,0:T(8,128)S(1)}, f32[2,3,128,128]{3,2,1,0:T(8,128)S(1)}, u32[]{:S(2)}, u32[]{:S(2)}) collective-permute-start(f32[2,3,128,128]{3,2,1,0:T(8,128)S(1)} %get-tuple-element.45), channel_id=1, source_target_pairs={{0,8},{8,0},{16,24},{24,16},{1,9},{9,1},{17,25},{25,17},{2,10},{10... | collective-permute-start | bytes 1179656 | tf_op jit(solution)/shard_map/ppermute | solution.py:412
  36.1 0.0 collective-permute-done.9.z1
  36.1 0.5 collective-permute-start.1
  36.6 1.5 %collective-permute-start.2 = (f32[2,3,128,128]{3,2,1,0:T(8,128)S(1)}, f32[2,3,128,128]{3,2,1,0:T(8,128)S(1)}, u32[]{:S(2)}, u32[]{:S(2)}) collective-permute-start(f32[2,3,128,128]{3,2,1,0:T(8,128)S(1)} %get-tuple-element.47), channel_id=1, source_target_pairs={{0,24},{8,16},{16,8},{24,0},{1,25},{9,17},{17,9},{25,1},{2,26},{10... | collective-permute-start | bytes 1179656 | tf_op jit(solution)/shard_map/ppermute | solution.py:412
  38.1 0.1 gather.1
  38.1 0.0 collective-permute-done.4.g2
  38.1 1.6 %collective-permute-start.12 = (f32[2,2,4,32,128]{4,3,2,1,0:T(8,128)S(1)}, f32[2,2,4,32,128]{4,3,2,1,0:T(8,128)S(1)}, u32[]{:S(2)}, u32[]{:S(2)}) collective-permute-start(f32[2,2,4,32,128]{4,3,2,1,0:T(8,128)S(1)} %get-tuple-element.62), channel_id=1, source_target_pairs={{0,8},{8,0},{16,24},{24,16},{1,9},{9,1},{17,25},{25,17},{2,10},{10... | collective-permute-start | bytes 786440 | tf_op jit(solution)/shard_map/ppermute | solution.py:412
  39.7 3.2 %collective-permute-done.5.g3 = f32[2,3,128,128]{3,2,1,0:T(8,128)S(1)} collective-permute-done((f32[2,3,128,128]{3,2,1,0:T(8,128)S(1)}, f32[2,3,128,128]{3,2,1,0:T(8,128)S(1)}, u32[]{:S(2)}, u32[]{:S(2)}) %collective-permute-start.5) | collective-permute-done | bytes 393248 | tf_op jit(solution)/shard_map/ppermute | solution.py:412
  42.9 3.7 %first_rounds.2 = (s32[18,8,128]{2,1,0:T(8,128)S(1)}, s32[2,3,32,128]{3,2,1,0:T(8,128)S(1)}, f32[2,3,32,128]{3,2,1,0:T(8,128)S(1)}, f32[2,3,32,128]{3,2,1,0:T(8,128)S(1)}, f32[2,3,32,128]{3,2,1,0:T(8,128)S(1)}) custom-call(s32[4]{0:T(128)S(1)} %copy-done, s32[1]{0:T(128)} %bitcast.gx_ref, s32[1]{0:T(128)} %bitcast.1.gy_ref, ...), custom_call_target="tpu_custom_call" | custom-call | tf_op jit(solution)/shard_map/first_rounds/pallas_call | solution.py:480
  46.6 0.1 collective-permute-start.15
  46.7 4.7 %collective-permute-done.g1 = f32[2,3,128,128]{3,2,1,0:T(8,128)S(1)} collective-permute-done((f32[2,3,128,128]{3,2,1,0:T(8,128)S(1)}, f32[2,3,128,128]{3,2,1,0:T(8,128)S(1)}, u32[]{:S(2)}, u32[]{:S(2)}) %collective-permute-start) | collective-permute-done | bytes 393248 | tf_op jit(solution)/shard_map/ppermute | solution.py:412
  51.4 0.5 collective-permute-start.13
  51.9 4.5 %collective-permute-done.1.g2 = f32[2,3,128,128]{3,2,1,0:T(8,128)S(1)} collective-permute-done((f32[2,3,128,128]{3,2,1,0:T(8,128)S(1)}, f32[2,3,128,128]{3,2,1,0:T(8,128)S(1)}, u32[]{:S(2)}, u32[]{:S(2)}) %collective-permute-start.1) | collective-permute-done | bytes 393248 | tf_op jit(solution)/shard_map/ppermute | solution.py:412
  56.4 0.4 collective-permute-start.14
  56.9 2.9 %collective-permute-done.2.g3 = f32[2,3,128,128]{3,2,1,0:T(8,128)S(1)} collective-permute-done((f32[2,3,128,128]{3,2,1,0:T(8,128)S(1)}, f32[2,3,128,128]{3,2,1,0:T(8,128)S(1)}, u32[]{:S(2)}, u32[]{:S(2)}) %collective-permute-start.2) | collective-permute-done | bytes 393248 | tf_op jit(solution)/shard_map/ppermute | solution.py:412
  59.8 0.7 collective-permute-start.16
  60.5 0.0 collective-permute-done.15.g1
  60.5 1.9 %collective-permute-start.17 = (f32[2,3,32,128]{3,2,1,0:T(8,128)S(1)}, f32[2,3,32,128]{3,2,1,0:T(8,128)S(1)}, u32[]{:S(2)}, u32[]{:S(2)}) collective-permute-start(f32[2,3,32,128]{3,2,1,0:T(8,128)S(1)} %get-tuple-element.68), channel_id=1, source_target_pairs={{0,6},{1,7},{2,4},{3,5},{4,2},{5,3},{6,0},{7,1},{8,14},{9,15},{10,... | collective-permute-start | bytes 294920 | tf_op jit(solution)/shard_map/ppermute | solution.py:412
  62.3 3.7 %first_rounds.3 = (s32[18,8,128]{2,1,0:T(8,128)S(1)}, s32[2,3,32,128]{3,2,1,0:T(8,128)S(1)}, f32[2,3,32,128]{3,2,1,0:T(8,128)S(1)}, f32[2,3,32,128]{3,2,1,0:T(8,128)S(1)}, f32[2,3,32,128]{3,2,1,0:T(8,128)S(1)}) custom-call(s32[4]{0:T(128)S(1)} %copy-done, s32[1]{0:T(128)} %bitcast.gx_ref, s32[1]{0:T(128)} %bitcast.1.gy_ref, ...), custom_call_target="tpu_custom_call", output_to_operand_aliasing={{0}: (8, {})} | custom-call | tf_op jit(solution)/shard_map/first_rounds/pallas_call | solution.py:480
  66.1 1.6 %collective-permute-done.16.g2 = f32[2,3,32,128]{3,2,1,0:T(8,128)S(1)} collective-permute-done((f32[2,3,32,128]{3,2,1,0:T(8,128)S(1)}, f32[2,3,32,128]{3,2,1,0:T(8,128)S(1)}, u32[]{:S(2)}, u32[]{:S(2)}) %collective-permute-start.16) | collective-permute-done | bytes 98336 | tf_op jit(solution)/shard_map/ppermute | solution.py:412
  67.6 0.0 collective-permute-start.6
  67.6 0.0 collective-permute-done.17.g3
  67.6 3.2 %collective-permute-start.7 = (f32[2,3,32,128]{3,2,1,0:T(8,128)S(1)}, f32[2,3,32,128]{3,2,1,0:T(8,128)S(1)}, u32[]{:S(2)}, u32[]{:S(2)}) collective-permute-start(f32[2,3,32,128]{3,2,1,0:T(8,128)S(1)} %get-tuple-element.56), channel_id=1, source_target_pairs={{0,4},{1,5},{2,6},{3,7},{4,0},{5,1},{6,2},{7,3},{8,12},{9,13},{10,... | collective-permute-start | bytes 294920 | tf_op jit(solution)/shard_map/ppermute | solution.py:412
  70.8 0.0 collective-permute-done.12.g1
  70.8 1.2 %collective-permute-start.8 = (f32[2,3,32,128]{3,2,1,0:T(8,128)S(1)}, f32[2,3,32,128]{3,2,1,0:T(8,128)S(1)}, u32[]{:S(2)}, u32[]{:S(2)}) collective-permute-start(f32[2,3,32,128]{3,2,1,0:T(8,128)S(1)} %get-tuple-element.57), channel_id=1, source_target_pairs={{0,6},{1,7},{2,4},{3,5},{4,2},{5,3},{6,0},{7,1},{8,14},{9,15},{10,... | collective-permute-start | bytes 294920 | tf_op jit(solution)/shard_map/ppermute | solution.py:412
  72.0 1.4 %shard_map.58 = (s32[18,8,128]{2,1,0:T(8,128)S(1)}, f32[3,8,32,128]{3,2,1,0:T(8,128)S(1)}, f32[3,8,32,128]{3,2,1,0:T(8,128)S(1)}) custom-call(s32[4]{0:T(128)S(1)} %copy-done, s32[1]{0:T(128)} %bitcast.gx_ref, s32[1]{0:T(128)} %bitcast.1.gy_ref, s32[2,3,32,128]{3,2,1,0:T(8,128)S(1)} %get-tuple-element.65.kept_ref, ...), custom_call_target="tpu_custom_call", output_to_operand_aliasing={{0}: (7, {})} | custom-call | tf_op jit(solution)/shard_map/pallas_call | solution.py:500
  73.5 3.3 %shard_map.59 = (s32[18,8,128]{2,1,0:T(8,128)S(1)}, f32[3,8,32,128]{3,2,1,0:T(8,128)S(1)}, f32[3,8,32,128]{3,2,1,0:T(8,128)S(1)}) custom-call(s32[4]{0:T(128)S(1)} %copy-done, s32[1]{0:T(128)} %bitcast.gx_ref, s32[1]{0:T(128)} %bitcast.1.gy_ref, ...), custom_call_target="tpu_custom_call", output_to_operand_aliasing={{0}: (10, {}), {1}: (11, {}), {2}: (12, {})} | custom-call | tf_op jit(solution)/shard_map/pallas_call | solution.py:500
  76.7 0.9 collective-permute-done.7.g2
  77.6 0.0 collective-permute-done.8.g3
  77.6 2.4 %shard_map.60 = (s32[18,8,128]{2,1,0:T(8,128)S(1)}, f32[3,8,32,128]{3,2,1,0:T(8,128)S(1)}, f32[3,8,32,128]{3,2,1,0:T(8,128)S(1)}, f32[32,1,128]{2,1,0:T(1,128)S(...) custom-call(s32[4]{0:T(128)S(1)} %copy-done, ...), custom_call_target="tpu_custom_call", output_to_operand_aliasing={{0}: (7, {}), {1}: (8, {}), {2}: (9, {})} | custom-call | tf_op jit(solution)/shard_map/pallas_call | solution.py:500
  80.1 10.1 %all_to_all.5 = f32[32,1,128]{2,1,0:T(1,128)S(1)} all-to-all(f32[32,1,128]{2,1,0:T(1,128)S(1)} %get-tuple-element.76), channel_id=1, replica_groups=mesh['gx'=4,'gy'=8] {'gx','gy'}, dimensions={0} | all-to-all | bytes 32768 | tf_op jit(solution)/shard_map/all_to_all | solution.py:557
  90.2 0.1 reduce_sum.11
  90.3 0.1 subtract_add_fusion.6
  90.4 0.1 subtract_add_fusion.5
  90.5 0.1 stack.12
  90.6 0.1 stack.13
  90.7 0.1 stack.14
  90.7 0.6 pad_maximum_fusion
  (9 shorter events, 0.1 us)
Async XLA Ops:
  3.0 33.6 %collective-permute-start.3 = (f32[2,3,128,128]{3,2,1,0:T(8,128)S(1)}, f32[2,3,128,128]{3,2,1,0:T(8,128)S(1)}, u32[]{:S(2)}, u32[]{:S(2)}) collective-permute-start(f32[2,3,128,128]{3,2,1,0:T(8,128)S(1)} %get-tuple-element.50), channel_id=1, source_target_pairs={{0,8},{8,0},{16,24},{24,16},{1,9},{9,1},{17,25},{25,17},{2,10},{10... | collective-permute-start | bytes 1179656 | tf_op jit(solution)/shard_map/ppermute | solution.py:412
  8.9 21.1 %collective-permute-start.10 = (f32[2,2,4,32,128]{4,3,2,1,0:T(8,128)S(1)}, f32[2,2,4,32,128]{4,3,2,1,0:T(8,128)S(1)}, u32[]{:S(2)}, u32[]{:S(2)}) collective-permute-start(f32[2,2,4,32,128]{4,3,2,1,0:T(8,128)S(1)} %get-tuple-element.60), channel_id=1, source_target_pairs={{0,4},{1,5},{2,6},{3,7},{4,0},{5,1},{6,2},{7,3},{8,12},{9,13},{10,... | collective-permute-start | bytes 786440 | tf_op jit(solution)/shard_map/ppermute | solution.py:412
  11.6 22.9 %collective-permute-start.11 = (f32[2,2,4,32,128]{4,3,2,1,0:T(8,128)S(1)}, f32[2,2,4,32,128]{4,3,2,1,0:T(8,128)S(1)}, u32[]{:S(2)}, u32[]{:S(2)}) collective-permute-start(f32[2,2,4,32,128]{4,3,2,1,0:T(8,128)S(1)} %get-tuple-element.61), channel_id=1, source_target_pairs={{0,6},{1,7},{2,4},{3,5},{4,2},{5,3},{6,0},{7,1},{8,14},{9,15},{10,... | collective-permute-start | bytes 786440 | tf_op jit(solution)/shard_map/ppermute | solution.py:412
  12.9 23.2 %collective-permute-start.9 = (f32[2,2,4,32,128]{4,3,2,1,0:T(8,128)S(1)}, f32[2,2,4,32,128]{4,3,2,1,0:T(8,128)S(1)}, u32[]{:S(2)}, u32[]{:S(2)}) collective-permute-start(f32[2,2,4,32,128]{4,3,2,1,0:T(8,128)S(1)} %get-tuple-element.59), channel_id=1, source_target_pairs={{0,2},{1,3},{2,0},{3,1},{4,6},{5,7},{6,4},{7,5},{8,10},{9,11},{10,... | collective-permute-start | bytes 786440 | tf_op jit(solution)/shard_map/ppermute | solution.py:412
  13.1 25.0 %collective-permute-start.4 = (f32[2,3,128,128]{3,2,1,0:T(8,128)S(1)}, f32[2,3,128,128]{3,2,1,0:T(8,128)S(1)}, u32[]{:S(2)}, u32[]{:S(2)}) collective-permute-start(f32[2,3,128,128]{3,2,1,0:T(8,128)S(1)} %get-tuple-element.51), channel_id=1, source_target_pairs={{0,16},{8,24},{16,0},{24,8},{1,17},{9,25},{17,1},{25,9},{2,18},{10... | collective-permute-start | bytes 1179656 | tf_op jit(solution)/shard_map/ppermute | solution.py:412
  30.0 12.9 %collective-permute-start.5 = (f32[2,3,128,128]{3,2,1,0:T(8,128)S(1)}, f32[2,3,128,128]{3,2,1,0:T(8,128)S(1)}, u32[]{:S(2)}, u32[]{:S(2)}) collective-permute-start(f32[2,3,128,128]{3,2,1,0:T(8,128)S(1)} %get-tuple-element.52), channel_id=1, source_target_pairs={{0,24},{8,16},{16,8},{24,0},{1,25},{9,17},{17,9},{25,1},{2,26},{10... | collective-permute-start | bytes 1179656 | tf_op jit(solution)/shard_map/ppermute | solution.py:412
  31.5 11.4 %copy-start = (s32[4]{0:T(128)S(1)}, s32[4]{0:T(128)}, u32[]{:S(2)}) copy-start(s32[4]{0:T(128)} %challenges_ref.9) | copy-start | bytes 52
  34.5 16.9 %collective-permute-start = (f32[2,3,128,128]{3,2,1,0:T(8,128)S(1)}, f32[2,3,128,128]{3,2,1,0:T(8,128)S(1)}, u32[]{:S(2)}, u32[]{:S(2)}) collective-permute-start(f32[2,3,128,128]{3,2,1,0:T(8,128)S(1)} %get-tuple-element.45), channel_id=1, source_target_pairs={{0,8},{8,0},{16,24},{24,16},{1,9},{9,1},{17,25},{25,17},{2,10},{10... | collective-permute-start | bytes 1179656 | tf_op jit(solution)/shard_map/ppermute | solution.py:412
  36.1 20.4 %collective-permute-start.1 = (f32[2,3,128,128]{3,2,1,0:T(8,128)S(1)}, f32[2,3,128,128]{3,2,1,0:T(8,128)S(1)}, u32[]{:S(2)}, u32[]{:S(2)}) collective-permute-start(f32[2,3,128,128]{3,2,1,0:T(8,128)S(1)} %get-tuple-element.46), channel_id=1, source_target_pairs={{0,16},{8,24},{16,0},{24,8},{1,17},{9,25},{17,1},{25,9},{2,18},{10... | collective-permute-start | bytes 1179656 | tf_op jit(solution)/shard_map/ppermute | solution.py:412
  36.6 23.2 %collective-permute-start.2 = (f32[2,3,128,128]{3,2,1,0:T(8,128)S(1)}, f32[2,3,128,128]{3,2,1,0:T(8,128)S(1)}, u32[]{:S(2)}, u32[]{:S(2)}) collective-permute-start(f32[2,3,128,128]{3,2,1,0:T(8,128)S(1)} %get-tuple-element.47), channel_id=1, source_target_pairs={{0,24},{8,16},{16,8},{24,0},{1,25},{9,17},{17,9},{25,1},{2,26},{10... | collective-permute-start | bytes 1179656 | tf_op jit(solution)/shard_map/ppermute | solution.py:412
  38.1 32.7 %collective-permute-start.12 = (f32[2,2,4,32,128]{4,3,2,1,0:T(8,128)S(1)}, f32[2,2,4,32,128]{4,3,2,1,0:T(8,128)S(1)}, u32[]{:S(2)}, u32[]{:S(2)}) collective-permute-start(f32[2,2,4,32,128]{4,3,2,1,0:T(8,128)S(1)} %get-tuple-element.62), channel_id=1, source_target_pairs={{0,8},{8,0},{16,24},{24,16},{1,9},{9,1},{17,25},{25,17},{2,10},{10... | collective-permute-start | bytes 786440 | tf_op jit(solution)/shard_map/ppermute | solution.py:412
  46.6 13.8 %collective-permute-start.15 = (f32[2,3,32,128]{3,2,1,0:T(8,128)S(1)}, f32[2,3,32,128]{3,2,1,0:T(8,128)S(1)}, u32[]{:S(2)}, u32[]{:S(2)}) collective-permute-start(f32[2,3,32,128]{3,2,1,0:T(8,128)S(1)} %get-tuple-element.66), channel_id=1, source_target_pairs={{0,2},{1,3},{2,0},{3,1},{4,6},{5,7},{6,4},{7,5},{8,10},{9,11},{10,... | collective-permute-start | bytes 294920 | tf_op jit(solution)/shard_map/ppermute | solution.py:412
  51.4 22.0 %collective-permute-start.13 = (f32[2,2,4,32,128]{4,3,2,1,0:T(8,128)S(1)}, f32[2,2,4,32,128]{4,3,2,1,0:T(8,128)S(1)}, u32[]{:S(2)}, u32[]{:S(2)}) collective-permute-start(f32[2,2,4,32,128]{4,3,2,1,0:T(8,128)S(1)} %get-tuple-element.63), channel_id=1, source_target_pairs={{0,16},{8,24},{16,0},{24,8},{1,17},{9,25},{17,1},{25,9},{2,18},{10... | collective-permute-start | bytes 786440 | tf_op jit(solution)/shard_map/ppermute | solution.py:412
  56.4 17.0 %collective-permute-start.14 = (f32[2,2,4,32,128]{4,3,2,1,0:T(8,128)S(1)}, f32[2,2,4,32,128]{4,3,2,1,0:T(8,128)S(1)}, u32[]{:S(2)}, u32[]{:S(2)}) collective-permute-start(f32[2,2,4,32,128]{4,3,2,1,0:T(8,128)S(1)} %get-tuple-element.64), channel_id=1, source_target_pairs={{0,24},{8,16},{16,8},{24,0},{1,25},{9,17},{17,9},{25,1},{2,26},{10... | collective-permute-start | bytes 786440 | tf_op jit(solution)/shard_map/ppermute | solution.py:412
  59.8 7.8 %collective-permute-start.16 = (f32[2,3,32,128]{3,2,1,0:T(8,128)S(1)}, f32[2,3,32,128]{3,2,1,0:T(8,128)S(1)}, u32[]{:S(2)}, u32[]{:S(2)}) collective-permute-start(f32[2,3,32,128]{3,2,1,0:T(8,128)S(1)} %get-tuple-element.67), channel_id=1, source_target_pairs={{0,4},{1,5},{2,6},{3,7},{4,0},{5,1},{6,2},{7,3},{8,12},{9,13},{10,... | collective-permute-start | bytes 294920 | tf_op jit(solution)/shard_map/ppermute | solution.py:412
  60.5 7.2 %collective-permute-start.17 = (f32[2,3,32,128]{3,2,1,0:T(8,128)S(1)}, f32[2,3,32,128]{3,2,1,0:T(8,128)S(1)}, u32[]{:S(2)}, u32[]{:S(2)}) collective-permute-start(f32[2,3,32,128]{3,2,1,0:T(8,128)S(1)} %get-tuple-element.68), channel_id=1, source_target_pairs={{0,6},{1,7},{2,4},{3,5},{4,2},{5,3},{6,0},{7,1},{8,14},{9,15},{10,... | collective-permute-start | bytes 294920 | tf_op jit(solution)/shard_map/ppermute | solution.py:412
  67.6 9.1 %collective-permute-start.6 = (f32[2,3,32,128]{3,2,1,0:T(8,128)S(1)}, f32[2,3,32,128]{3,2,1,0:T(8,128)S(1)}, u32[]{:S(2)}, u32[]{:S(2)}) collective-permute-start(f32[2,3,32,128]{3,2,1,0:T(8,128)S(1)} %get-tuple-element.55), channel_id=1, source_target_pairs={{0,2},{1,3},{2,0},{3,1},{4,6},{5,7},{6,4},{7,5},{8,10},{9,11},{10,... | collective-permute-start | bytes 294920 | tf_op jit(solution)/shard_map/ppermute | solution.py:412
  67.6 10.0 %collective-permute-start.7 = (f32[2,3,32,128]{3,2,1,0:T(8,128)S(1)}, f32[2,3,32,128]{3,2,1,0:T(8,128)S(1)}, u32[]{:S(2)}, u32[]{:S(2)}) collective-permute-start(f32[2,3,32,128]{3,2,1,0:T(8,128)S(1)} %get-tuple-element.56), channel_id=1, source_target_pairs={{0,4},{1,5},{2,6},{3,7},{4,0},{5,1},{6,2},{7,3},{8,12},{9,13},{10,... | collective-permute-start | bytes 294920 | tf_op jit(solution)/shard_map/ppermute | solution.py:412
  70.8 6.8 %collective-permute-start.8 = (f32[2,3,32,128]{3,2,1,0:T(8,128)S(1)}, f32[2,3,32,128]{3,2,1,0:T(8,128)S(1)}, u32[]{:S(2)}, u32[]{:S(2)}) collective-permute-start(f32[2,3,32,128]{3,2,1,0:T(8,128)S(1)} %get-tuple-element.57), channel_id=1, source_target_pairs={{0,6},{1,7},{2,4},{3,5},{4,2},{5,3},{6,0},{7,1},{8,14},{9,15},{10,... | collective-permute-start | bytes 294920 | tf_op jit(solution)/shard_map/ppermute | solution.py:412

commit v2 on v1

--- a/solution.py
+++ b/solution.py
@@ -111,12 +111,12 @@
             acc_ref[5 * kind + n] = jnp.zeros((8, LANES), jnp.int32)
 
 
-def two_rounds(acc_ref, splat_ref, s, w):
+def two_rounds(acc_ref, weights_ref, phase, s, w):
     s, w = [[x if isinstance(x, tuple) else limbs_of(x) for x in v] for v in (s, w)]
     for kind, (a, b) in enumerate(zip(nine_of(s), nine_of(w))):
         for n, d in enumerate(degrees(a, b)):
             acc_ref[5 * kind + n] = acc_ref[5 * kind + n] + d
-    weights = [[splat_ref[6 * x + n] for n in range(6)] for x in range(4)]
+    weights = [[weights_ref[24 * phase + 6 * x + n] for n in range(6)] for x in range(4)]
     return weighted_sum(s, weights), weighted_sum(w, weights)
 
 
@@ -163,71 +163,86 @@
     return [x & 65535 for x in parts] + [shr(x, 16) for x in parts]
 
 
-def splat_weights(challenges_ref, place, phase, splat_ref):
-    first, second = sides(challenges_ref, place, phase)
-    for x in range(4):
-        for n, c in enumerate(constants_of(mul_mod(first[x >> 1], second[x & 1]))):
-            splat_ref[6 * x + n] = c
+SQUARES, LOW_SIDE, WEIGHTS = 48, 84, 88
+
+
+def place_of(axis):
+    return lax.axis_index(axis) >> (lax.axis_size(axis).bit_length() - 3)
+
+
+def weights_kernel(challenges_ref, weights_ref):
+    for phase, axis in enumerate(("gx", "gy")):
+        place = place_of(axis)
+        first, second = sides(challenges_ref, place, phase)
+        for x in range(4):
+            for n, c in enumerate(constants_of(mul_mod(first[x >> 1], second[x & 1]))):
+                weights_ref[24 * phase + 6 * x + n] = c
+        own, other = first
+        for x, pair in enumerate(((own, own), (own, other), (other, other))):
+            for n, c in enumerate(constants_of(mul_mod(*pair))):
+                weights_ref[SQUARES + 18 * phase + 6 * x + n] = c
+        for k in range(2):
+            weights_ref[LOW_SIDE + 2 * phase + k] = whole((place >> (1 - k)) & 1)
 
 
 def tile(start, i):
     return pl.ds(pl.multiple_of(start + i * 8, 8), 8)
 
 
-def start_owns(owns, place, tables, outs, sems):
-    copies = []
-    for n, (start, count) in enumerate(owns):
-        for t in range(2):
-            out = outs[2 * n + t]
-            rows = out.shape[2]
-            src = tables[t].at[:, pl.ds(start, count), pl.ds(pl.multiple_of(place * rows, rows), rows), :]
-            copies.append(pltpu.make_async_copy(src, out, sems.at[n, t]))
-    for copy in copies:
-        copy.start()
-    return copies
-
-
-def encode_kernel(raw, start, owns, gx_ref, gy_ref, s_hbm, w_hbm, *refs):
+def over_tiles(rows, step):
+    lax.fori_loop(0, rows // 8, step, None, unroll=min(UNROLL, rows // 8))
+
+
+def item_of(table, item, quarter):
+    parts = table.shape[4]
+    return table.at[:, item // parts, quarter, :, item % parts]
+
+
+def encode_kernel(raw, start, owns, s_hbm, w_hbm, *refs):
+    tables = (s_hbm, w_hbm)
+    gx, gy = place_of("gx"), place_of("gy")
+    own_copies = []
     if len(owns):
         refs, own_sems = refs[:-1], refs[-1]
     buffer, sems = refs[-2:]
     refs = refs[:-2]
     if len(owns):
         refs, own_outs = refs[: -2 * len(owns)], refs[-2 * len(owns) :]
+        own_copies = [
+            pltpu.make_async_copy(item_of(tables[t], first + i, gx), own_outs[2 * n + t].at[:, i], own_sems.at[n, i, t])
+            for n, (first, count) in enumerate(owns)
+            for i in range(count)
+            for t in range(2)
+        ]
     token_ref = refs[-1]
     outs = refs[-5:-1] if raw else refs[-4:-1]
-    count, rows = buffer.shape[0], buffer.shape[4]
+    count, rows = buffer.shape[0], buffer.shape[5]
     shifts = (1, 2, 3, 0) if raw else (1, 2, 3)
-    order = [(j, d, t) for j in range(count) for d in shifts for t in range(2)]
-
-    def copy(j, d, t):
-        src = (s_hbm, w_hbm)[t].at[:, start + j, pl.ds(pl.multiple_of((gx_ref[0] ^ d) * rows, rows), rows), :]
-        return pltpu.make_async_copy(src, buffer.at[j, d % len(shifts), t], sems.at[j, d % len(shifts), t])
+    order = [(i, d, t) for i in range(count) for d in shifts for t in range(2)]
+
+    def copy(i, d, t):
+        slot = d % len(shifts)
+        return pltpu.make_async_copy(item_of(tables[t], start + i, gx ^ d), buffer.at[i, slot, t], sems.at[i, slot, t])
 
     for where in order:
         copy(*where).start()
-    if len(owns):
-        own_copies = start_owns(owns, gx_ref[0], (s_hbm, w_hbm), own_outs, own_sems)
+    for copy_own in own_copies:
+        copy_own.start()
     token_ref[...] = jnp.zeros_like(token_ref)
-    sub = rows // 4
     for where in order:
-        j, d, t = where
-        slot = d % len(shifts)
+        i, d, t = where
         copy(*where).wait()
-        for e in range(4 if raw else 1):
-            first = (gy_ref[0] ^ e) * sub if raw else 0
-
-            def step(i, _):
-                word = word_of_limbs(*[buffer[j, slot, t, n, tile(first, i)] for n in range(3)])
+        for e in range(4):
+            src = gy ^ e if raw else e
+            for k in range(rows // 8):
+                at = pl.ds(8 * k, 8)
+                word = word_of_limbs(*[buffer[i, d % len(shifts), t, n, src, at] for n in range(3)])
                 if raw:
-                    outs[e][t, j, d, tile(0, i)] = word
+                    outs[e][t, i, d, at] = word
                 else:
-                    outs[d - 1][t, j, tile(0, i)] = word
-
-            lax.fori_loop(0, (sub if raw else rows) // 8, step, None, unroll=4)
-    if len(owns):
-        for copy_own in own_copies:
-            copy_own.wait()
+                    outs[d - 1][t, i, e, at] = word
+    for copy_own in own_copies:
+        copy_own.wait()
 
 
 def gather_kernel(z0, z1, z2, z3, o1, o2, o3):
@@ -238,32 +253,31 @@
                     out[t, j, e] = src[t, j, d + 1]
 
 
-def first_kernel(fresh, challenges_ref, gx_ref, gy_ref, s_ref, w_ref, g1, g2, g3, *refs):
+def first_kernel(fresh, weights_ref, s_ref, w_ref, g1, g2, g3, *refs):
     if not fresh:
         before_ref, *refs = refs
-    points_ref, kept_ref, o1, o2, o3, acc_ref, splat_ref = refs
-    count, rows = s_ref.shape[1], s_ref.shape[2]
-    sub = rows // 4
+    points_ref, kept_ref, o1, o2, o3, acc_ref = refs
+    count, rows = s_ref.shape[1], s_ref.shape[3]
     given, outs = (g1, g2, g3), (kept_ref, o1, o2, o3)
-    splat_weights(challenges_ref, gx_ref[0], 0, splat_ref)
+    gy = place_of("gy")
     points_ref[...] = jnp.zeros_like(points_ref) if fresh else before_ref[...]
 
     def pair(j):
         for e in range(4):
-            start = (gy_ref[0] ^ e) * sub
+            src = gy ^ e
 
             def step(i, _):
-                at = tile(start, i)
+                at = tile(0, i)
                 values = []
                 for t, own in enumerate((s_ref, w_ref)):
-                    limbs = tuple(own[n, j, at].astype(jnp.int32) for n in range(3))
-                    values.append([limbs] + [int_of_word(g[t, j, at]) for g in given])
-                for t, folded in enumerate(two_rounds(acc_ref, splat_ref, *values)):
-                    outs[e][t, j, tile(0, i)] = word_of_int(folded) if e else folded
-
-            lax.fori_loop(0, sub // 8, step, None, unroll=UNROLL)
-
-    over_pairs(count, rows // 8, [(acc_ref, points_ref, 0)], pair)
+                    limbs = tuple(own[n, j, src, at].astype(jnp.int32) for n in range(3))
+                    values.append([limbs] + [int_of_word(g[t, j, src, at]) for g in given])
+                for t, folded in enumerate(two_rounds(acc_ref, weights_ref, 0, *values)):
+                    outs[e][t, j, at] = word_of_int(folded) if e else folded
+
+            over_tiles(rows, step)
+
+    over_pairs(count, rows // 2, [(acc_ref, points_ref, 0)], pair)
 
 
 def settle(lowest, middle, highest, passes=3):
@@ -283,9 +297,8 @@
     return [jnp.where(at_modulus, 0.0, limb) for limb in (lowest, middle, highest)]
 
 
-def round_sums(challenges_ref, place, phase, points):
-    own, other = sides(challenges_ref, place, phase)[0]
-    squares = [constants_of(mul_mod(*x)) for x in ((own, own), (own, other), (other, other))]
+def round_sums(weights_ref, phase, points):
+    squares = [[weights_ref[SQUARES + 18 * phase + 6 * x + n] for n in range(6)] for x in range(3)]
     i0, i1, i2, i3, i02, i13, i01, i23, i0123 = points
     first = [add_mod(i0, i1), add_mod(i2, i3), add_mod(i02, i13)]
     second = []
@@ -295,14 +308,13 @@
     return [first, second]
 
 
-def publish_row(challenges_ref, places, points_ref, sums_ref):
+def publish_row(weights_ref, points_ref, sums_ref):
     lane = lax.broadcasted_iota(jnp.int32, (1, LANES), 1)
     rows = [jnp.zeros((1, LANES), jnp.float32) for _ in range(3)]
     for phase in range(2):
-        place = places[phase]
         points = [points_ref[9 * phase + n] for n in range(9)]
-        for k, (own, other, both) in enumerate(round_sums(challenges_ref, place, phase, points)):
-            is_low = whole((place >> (1 - k)) & 1) == 0
+        for k, (own, other, both) in enumerate(round_sums(weights_ref, phase, points)):
+            is_low = weights_ref[LOW_SIDE + 2 * phase + k] == 0
             at_zero = jnp.where(is_low, own, other)
             at_one = jnp.where(is_low, other, own)
             once = add_mod(at_zero, add_mod(at_one, at_one))
@@ -332,9 +344,9 @@
         for copy in self.parts[which]:
             copy.start()
 
-    def end(self, challenges_ref, places, points_ref):
+    def end(self, weights_ref, points_ref):
         self.start(1)
-        publish_row(challenges_ref, places, points_ref, self.sums_ref)
+        publish_row(weights_ref, points_ref, self.sums_ref)
         for copy in self.parts[0] + self.parts[1]:
             copy.wait()
 
@@ -345,44 +357,41 @@
             out[n, j, at] = limb.astype(jnp.float32)
 
 
-def second_kernel(start, fresh, last, challenges_ref, gx_ref, gy_ref, kept_ref, g1, g2, g3, before_ref, *refs):
+def second_kernel(start, fresh, last, weights_ref, kept_ref, g1, g2, g3, before_ref, *refs):
     if not fresh:
         refs = refs[2:]
     points_ref, s_ref, w_ref, *refs = refs
     count, rows = kept_ref.shape[1], kept_ref.shape[2]
     if last:
-        finish = Finish((0, start), (start, count), s_ref, w_ref, refs[:3] + refs[5:])
-        refs = refs[3:5]
-    acc_ref, splat_ref = refs
+        finish = Finish((0, start), (start, count), s_ref, w_ref, refs[:3] + refs[4:])
+        refs = refs[3:4]
+    (acc_ref,) = refs
     given = (g1, g2, g3)
-    splat_weights(challenges_ref, gy_ref[0], 1, splat_ref)
     points_ref[...] = before_ref[...]
 
     def pair(j):
         def step(i, _):
             at = tile(0, i)
             s, w = [[kept_ref[t, j, at]] + [int_of_word(g[t, j, at]) for g in given] for t in range(2)]
-            put_folded((s_ref, w_ref), start + j, at, two_rounds(acc_ref, splat_ref, s, w))
-
-        lax.fori_loop(0, rows // 8, step, None, unroll=UNROLL)
+            put_folded((s_ref, w_ref), start + j, at, two_rounds(acc_ref, weights_ref, 1, s, w))
+
+        over_tiles(rows, step)
 
     over_pairs(count, rows // 8, [(acc_ref, points_ref, 9)], pair)
     if last:
-        finish.end(challenges_ref, (gx_ref[0], gy_ref[0]), points_ref)
-
-
-def all_kernel(start, fresh, last, challenges_ref, gx_ref, gy_ref, z0, z1, z2, z3, g1, g2, g3, before_ref, *refs):
+        finish.end(weights_ref, points_ref)
+
+
+def all_kernel(start, fresh, last, weights_ref, z0, z1, z2, z3, g1, g2, g3, before_ref, *refs):
     if not fresh:
         refs = refs[2:]
     points_ref, s_ref, w_ref, *refs = refs
     count, rows = z0.shape[1], z0.shape[3]
     if last:
-        finish = Finish((0, start), (start, count), s_ref, w_ref, refs[:3] + refs[5 + 3 :])
-        refs = refs[3 : 5 + 3]
-    acc_ref, splat_ref, acc2_ref, splat2_ref, once = refs
+        finish = Finish((0, start), (start, count), s_ref, w_ref, refs[:3] + refs[6:])
+        refs = refs[3:6]
+    acc_ref, acc2_ref, once = refs
     given = (g1, g2, g3)
-    splat_weights(challenges_ref, gx_ref[0], 0, splat_ref)
-    splat_weights(challenges_ref, gy_ref[0], 1, splat2_ref)
     points_ref[...] = before_ref[...]
 
     def pair(j):
@@ -391,57 +400,54 @@
             def step(i, _):
                 at = tile(0, i)
                 s, w = [[int_of_word(x) for x in [own[t, j, 0, at]] + [g[t, j, e, at] for g in given]] for t in range(2)]
-                for t, folded in enumerate(two_rounds(acc_ref, splat_ref, s, w)):
+                for t, folded in enumerate(two_rounds(acc_ref, weights_ref, 0, s, w)):
                     once[t, e, at] = folded
 
-            lax.fori_loop(0, rows // 8, step, None, unroll=UNROLL)
+            over_tiles(rows, step)
 
         def step(i, _):
             at = tile(0, i)
             s, w = [[once[t, e, at] for e in range(4)] for t in range(2)]
-            put_folded((s_ref, w_ref), start + j, at, two_rounds(acc2_ref, splat2_ref, s, w))
-
-        lax.fori_loop(0, rows // 8, step, None, unroll=UNROLL)
+            put_folded((s_ref, w_ref), start + j, at, two_rounds(acc2_ref, weights_ref, 1, s, w))
+
+        over_tiles(rows, step)
 
     over_pairs(count, rows // 2, [(acc_ref, points_ref, 0), (acc2_ref, points_ref, 9)], pair)
     if last:
-        finish.end(challenges_ref, (gx_ref[0], gy_ref[0]), points_ref)
+        finish.end(weights_ref, points_ref)
 
 
 def swap_with(x, axis, mask):
     return lax.ppermute(x, axis, [(i, i ^ mask) for i in range(lax.axis_size(axis))])
 
 
-CHUNKS, RAW = (3, 3), 2
+SPLIT = 1
+CHUNKS, RAW = (4, 2), 2
 SENDS = "0R1"
 STEPS = ("A0", "G", "A1", "B0", "K", "B1")
 POINTS = pltpu.VMEM((18, 8, LANES), jnp.int32)
 
 
-def plan(polynomials):
-    if sum(CHUNKS) + RAW == polynomials:
+def plan(items):
+    if sum(CHUNKS) + RAW == items:
         return CHUNKS, RAW, SENDS, STEPS
-    sizes = (1,) * polynomials
-    steps = ["A0"] + [x for c in range(1, polynomials) for x in (f"A{c}", f"B{c - 1}")] + [f"B{polynomials - 1}"]
-    return sizes, 0, range(polynomials), steps
+    steps = ["A0"] + [x for c in range(1, items) for x in (f"A{c}", f"B{c - 1}")] + [f"B{items - 1}"]
+    return (1,) * items, 0, range(items), steps
 
 
 def shards(devices, selectors, proofs, challenges):
     polynomials, row_count = selectors.shape[1], selectors.shape[-1]
     lane_rows = row_count // LANES
-    quarter, final = lane_rows // 4, lane_rows // 16
-    tables = [
-        pltpu.with_memory_space_constraint(x.reshape(3, polynomials, lane_rows, LANES), pltpu.HBM)
-        for x in (selectors, proofs)
-    ]
+    parts = SPLIT if lane_rows % (128 * SPLIT) == 0 else 1
+    items, final = polynomials * parts, lane_rows // 16 // parts
+    shape = (3, polynomials, 4, 4, parts, final, LANES)
+    tables = [pltpu.with_memory_space_constraint(x.reshape(shape), pltpu.HBM) for x in (selectors, proofs)]
     gx_shift = lax.axis_size("gx").bit_length() - 3
     gy_shift = lax.axis_size("gy").bit_length() - 3
-    gx_place = (lax.axis_index("gx") >> gx_shift).astype(jnp.int32).reshape(1)
-    gy_place = (lax.axis_index("gy") >> gy_shift).astype(jnp.int32).reshape(1)
-
-    sizes, raw, sends, steps = plan(polynomials)
+
+    sizes, raw, sends, steps = plan(items)
     raw_last = steps[-1] == "K"
-    raw_start = polynomials - raw if raw_last else 0
+    raw_start = items - raw if raw_last else 0
     starts = [sum(sizes[:c]) + (0 if raw_last else raw) for c in range(len(sizes))]
     smem, vmem, hbm, anywhere = [pl.BlockSpec(memory_space=m) for m in (pltpu.SMEM, pltpu.VMEM, pltpu.HBM, pl.ANY)]
 
@@ -451,61 +457,61 @@
     def near(arrays):
         return [pltpu.with_memory_space_constraint(x, pltpu.VMEM) for x in arrays]
 
-    work = [pltpu.VMEM((45, 8, LANES), jnp.int32), pltpu.VMEM((24, 8, LANES), jnp.int32)]
+    work = [pltpu.VMEM((45, 8, LANES), jnp.int32)]
     small = pltpu.CompilerParams(vmem_limit_bytes=VMEM_KERNEL)
 
     def encode(raw_chunk, start, count, outs, owns, token):
         out_shape = outs + [pltpu.VMEM((8, LANES), jnp.float32)]
-        out_shape += [pltpu.VMEM((3, n, quarter, LANES), jnp.float32) for _, n in owns for _ in range(2)]
+        out_shape += [pltpu.VMEM((3, n, 4, final, LANES), jnp.float32) for _, n in owns for _ in range(2)]
         shifts = 4 if raw_chunk else 3
         scratch = [
-            pltpu.VMEM((count, shifts, 2, 3, quarter, LANES), jnp.float32),
+            pltpu.VMEM((count, shifts, 2, 3, 4, final, LANES), jnp.float32),
             pltpu.SemaphoreType.DMA((count, shifts, 2)),
         ]
         if owns:
-            scratch.append(pltpu.SemaphoreType.DMA((len(owns), 2)))
+            scratch.append(pltpu.SemaphoreType.DMA((len(owns), max(n for _, n in owns), 2)))
         return pl.pallas_call(
             functools.partial(encode_kernel, raw_chunk, start, owns),
-            in_specs=[smem, smem, hbm, hbm] + [anywhere] * len(token),
+            in_specs=[hbm, hbm] + [anywhere] * len(token),
             out_specs=[vmem] * len(out_shape),
             out_shape=out_shape,
             scratch_shapes=scratch,
             compiler_params=pltpu.CompilerParams(vmem_limit_bytes=VMEM_ENCODE),
             name="encode",
-        )(gx_place, gy_place, *tables, *token)
+        )(*tables, *token)
 
     def first(c, own, given, before):
         count = sizes[c]
         fresh = before is None
         return pl.pallas_call(
             functools.partial(first_kernel, fresh),
-            in_specs=[smem] * 3 + [vmem] * (5 if fresh else 6),
+            in_specs=[vmem] * (6 if fresh else 7),
             out_specs=[vmem] * 5,
             out_shape=[POINTS, words(count, [final], jnp.int32)] + [words(count, [final])] * 3,
             scratch_shapes=work,
-            input_output_aliases={} if fresh else {8: 0},
+            input_output_aliases={} if fresh else {6: 0},
             compiler_params=small,
             name="first_rounds",
-        )(challenges, gx_place, gy_place, *own, *near(given), *(() if fresh else (before,)))
+        )(weights, *own, *near(given), *(() if fresh else (before,)))
 
     def fold_last(kernel, start, arrays, before, folded, last, scratch):
         fresh = folded is None
-        shape = (3, polynomials, final, LANES)
+        shape = (3, items, final, LANES)
         out_shape, out_specs = [POINTS] + [pltpu.VMEM(shape, jnp.float32)] * 2, [vmem] * 3
         if last:
             out_shape += [jax.ShapeDtypeStruct((devices, 1, LANES), jnp.float32)] + [jax.ShapeDtypeStruct(shape, jnp.float32)] * 2
             out_specs += [vmem, hbm, hbm]
             scratch = scratch + [pltpu.SemaphoreType.DMA((2, 2))]
-        at = 3 + len(arrays)
+        at = 1 + len(arrays)
         return pl.pallas_call(
             functools.partial(kernel, start, fresh, last),
-            in_specs=[smem] * 3 + [vmem] * (len(arrays) + (1 if fresh else 3)),
+            in_specs=[vmem] * (len(arrays) + (2 if fresh else 4)),
             out_specs=out_specs,
             out_shape=out_shape,
             scratch_shapes=scratch,
             input_output_aliases={at: 0} if fresh else {at: 0, at + 1: 1, at + 2: 2},
             compiler_params=small,
-        )(challenges, gx_place, gy_place, *near(arrays), before, *(() if fresh else folded))
+        )(weights, *near(arrays), before, *(() if fresh else folded))
 
     def swap(arrays, axis, shift):
         return [swap_with(x, axis, (d + 1) << shift) for d, x in enumerate(arrays)]
@@ -519,7 +525,7 @@
             start, count, outs = raw_start, raw, [words(raw, [4, final])] * 4
         else:
             start, count = ranges[int(c)]
-            outs = [words(count, [quarter])] * 3
+            outs = [words(count, [4, final])] * 3
         out = encode(raw_chunk, start, count, outs, ranges if c == reader else [], token)
         given, token = out[: len(outs)], [out[len(outs)]]
         if raw_chunk:
@@ -528,6 +534,14 @@
             rest = out[len(outs) + 1 :]
             owns = {n: rest[2 * n : 2 * n + 2] for n in range(len(ranges))}
         sent[c if raw_chunk else int(c)] = swap(given, *(("gy", gy_shift) if raw_chunk else ("gx", gx_shift)))
+    weights = pl.pallas_call(
+        weights_kernel,
+        in_specs=[smem],
+        out_specs=vmem,
+        out_shape=pltpu.VMEM((WEIGHTS, 8, LANES), jnp.int32),
+        compiler_params=small,
+        name="weights",
+    )(challenges)
     points, folded, waiting = None, None, {}
     for step in steps:
         last = step == steps[-1]

time: 91.5 us -> 84.7 us (0.926)
  waiting for transfers between devices: 33.2 us -> 29.1 us
  Pallas kernels: 22.8 us -> 20.5 us
    ppermute x18, waiting for transfers between devices: 33.2 us -> 29.1 us  [swap_with(): lax.ppermute(x, axis, [(i, i ^ mask) for i in range(lax.axis_size(axis))])]
    pallas_call x5 -> x6, Pallas kernels: 14.6 us -> 12.5 us  [the longest x2 6.45 us: first(): pl.pallas_call(functools.partial(first_kernel, fresh), in_specs=[vmem] *...]
  transfers between devices with their start and end apart: 18 -> 18, of which waited for: 7 -> 8; matrix products, arithmetic and copies ran while one was open for 0% -> 0% of each run, Pallas kernels for 20% -> 16%
where the time goes in v2:
time: 84.7 us; the launch traced here: 84.6 us
  waiting for transfers between devices  29.1 us (34%)
  starting transfers between devices  23.2 us (27%)
  Pallas kernels  20.5 us (24%)
  blocking collectives  9.85 us (12%)
  other arithmetic  0.87 us (1%)
    ppermute x18, waiting for transfers between devices, swap_with(): lax.ppermute(x, axis, [(i, i ^ mask) for i in range(lax.axis_size(axis))])  29.1 us
    ppermute x18, starting transfers between devices, swap_with(): lax.ppermute(x, axis, [(i, i ^ mask) for i in range(lax.axis_size(axis))])  23.2 us
    all_to_all x1, blocking collectives, shards(): gathered = lax.all_to_all(sums, ('gx', 'gy'), 0, 0)  9.85 us
    pallas_call x3, Pallas kernels, encode(): pl.pallas_call(functools.partial(encode_kernel, raw_chunk, start, owns),...  8.01 us
    pallas_call x2, Pallas kernels, first(): pl.pallas_call(functools.partial(first_kernel, fresh), in_specs=[vmem] *...  6.45 us
    pallas_call x3, Pallas kernels, fold_last(): pl.pallas_call(functools.partial(kernel, start, fresh, last), in_specs=[v...  5.32 us
  transfers between devices with their start and end apart: 18, of which 8 were waited for; matrix products, arithmetic and copies ran while one was open for 0% of the time, Pallas kernels for 16%

profile of v2, /device:TPU:0, one launch (start us, length us, event | category | flops | bytes accessed | tf_op | source)
XLA Modules:
  0.0 84.6 jit_solution(6502541518753924873)
XLA Ops:
  0.6 2.7 %encode.3 = (f32[2,4,4,32,128]{4,3,2,1,0:T(8,128)S(1)}, f32[2,4,4,32,128]{4,3,2,1,0:T(8,128)S(1)}, f32[2,4,4,32,128]{4,3,2,1,0:T(8,128)S(1)}, f32[8,128]{1,0:T(8,128)S(1)}) custom-call(f32[3,8,4,4,1,32,128]{6,5,4,3,2,1,0:T(8,128)} %bitcast.5, f32[3,8,4,4,1,32,128]{6,5,4,3,2,1,0:T(8,128)} %bitcast.8), custom_call_target="tpu_custom_call" | custom-call | tf_op jit(solution)/shard_map/encode/pallas_call | solution.py:473
  3.3 2.9 %encode.4 = (f32[2,2,4,32,128]{4,3,2,1,0:T(8,128)S(1)}, f32[2,2,4,32,128]{4,3,2,1,0:T(8,128)S(1)}, f32[2,2,4,32,128]{4,3,2,1,0:T(8,128)S(1)}, f32[2,2,4,32,128]{...) custom-call(f32[3,8,4,4,1,32,128]{6,5,4,3,2,1,0:T(8,128)} %bitcast.6, ...), custom_call_target="tpu_custom_call" | custom-call | tf_op jit(solution)/shard_map/encode/pallas_call | solution.py:473
  6.3 3.1 %collective-permute-start.9 = (f32[2,2,4,32,128]{4,3,2,1,0:T(8,128)S(1)}, f32[2,2,4,32,128]{4,3,2,1,0:T(8,128)S(1)}, u32[]{:S(2)}, u32[]{:S(2)}) collective-permute-start(f32[2,2,4,32,128]{4,3,2,1,0:T(8,128)S(1)} %get-tuple-element.59), channel_id=1, source_target_pairs={{0,2},{1,3},{2,0},{3,1},{4,6},{5,7},{6,4},{7,5},{8,10},{9,11},{10,... | collective-permute-start | bytes 786440 | tf_op jit(solution)/shard_map/ppermute | solution.py:421
  9.4 2.6 %collective-permute-start.10 = (f32[2,2,4,32,128]{4,3,2,1,0:T(8,128)S(1)}, f32[2,2,4,32,128]{4,3,2,1,0:T(8,128)S(1)}, u32[]{:S(2)}, u32[]{:S(2)}) collective-permute-start(f32[2,2,4,32,128]{4,3,2,1,0:T(8,128)S(1)} %get-tuple-element.60), channel_id=1, source_target_pairs={{0,4},{1,5},{2,6},{3,7},{4,0},{5,1},{6,2},{7,3},{8,12},{9,13},{10,... | collective-permute-start | bytes 786440 | tf_op jit(solution)/shard_map/ppermute | solution.py:421
  12.0 1.5 %collective-permute-start.3 = (f32[2,4,4,32,128]{4,3,2,1,0:T(8,128)S(1)}, f32[2,4,4,32,128]{4,3,2,1,0:T(8,128)S(1)}, u32[]{:S(2)}, u32[]{:S(2)}) collective-permute-start(f32[2,4,4,32,128]{4,3,2,1,0:T(8,128)S(1)} %get-tuple-element.50), channel_id=1, source_target_pairs={{0,8},{8,0},{16,24},{24,16},{1,9},{9,1},{17,25},{25,17},{2,10},{10... | collective-permute-start | bytes 1572872 | tf_op jit(solution)/shard_map/ppermute | solution.py:421
  13.5 1.5 %collective-permute-start.4 = (f32[2,4,4,32,128]{4,3,2,1,0:T(8,128)S(1)}, f32[2,4,4,32,128]{4,3,2,1,0:T(8,128)S(1)}, u32[]{:S(2)}, u32[]{:S(2)}) collective-permute-start(f32[2,4,4,32,128]{4,3,2,1,0:T(8,128)S(1)} %get-tuple-element.51), channel_id=1, source_target_pairs={{0,16},{8,24},{16,0},{24,8},{1,17},{9,25},{17,1},{25,9},{2,18},{10... | collective-permute-start | bytes 1572872 | tf_op jit(solution)/shard_map/ppermute | solution.py:421
  15.0 0.5 collective-permute-start.5
  15.5 5.7 %collective-permute-done.9.z1 = f32[2,2,4,32,128]{4,3,2,1,0:T(8,128)S(1)} collective-permute-done((f32[2,2,4,32,128]{4,3,2,1,0:T(8,128)S(1)}, f32[2,2,4,32,128]{4,3,2,1,0:T(8,128)S(1)}, u32[]{:S(2)}, u32[]{:S(2)}) %collective-permute-start.9) | collective-permute-done | bytes 262176 | tf_op jit(solution)/shard_map/ppermute | solution.py:421
  21.2 2.6 %collective-permute-start.11 = (f32[2,2,4,32,128]{4,3,2,1,0:T(8,128)S(1)}, f32[2,2,4,32,128]{4,3,2,1,0:T(8,128)S(1)}, u32[]{:S(2)}, u32[]{:S(2)}) collective-permute-start(f32[2,2,4,32,128]{4,3,2,1,0:T(8,128)S(1)} %get-tuple-element.61), channel_id=1, source_target_pairs={{0,6},{1,7},{2,4},{3,5},{4,2},{5,3},{6,0},{7,1},{8,14},{9,15},{10,... | collective-permute-start | bytes 786440 | tf_op jit(solution)/shard_map/ppermute | solution.py:421
  23.8 2.4 %encode.5 = (f32[2,2,4,32,128]{4,3,2,1,0:T(8,128)S(1)}, f32[2,2,4,32,128]{4,3,2,1,0:T(8,128)S(1)}, f32[2,2,4,32,128]{4,3,2,1,0:T(8,128)S(1)}, f32[8,128]{1,0:T(8,128)}) custom-call(f32[3,8,4,4,1,32,128]{6,5,4,3,2,1,0:T(8,128)} %bitcast.7, f32[3,8,4,4,1,32,128]{6,5,4,3,2,1,0:T(8,128)} %bitcast.10, f32[8,128]{1,0:T(8,128)S(1)} %get-tuple-element.44.refs_0_), custom_call_target="tpu_custom_call" | custom-call | tf_op jit(solution)/shard_map/encode/pallas_call | solution.py:473
  26.2 1.6 %collective-permute-start = (f32[2,2,4,32,128]{4,3,2,1,0:T(8,128)S(1)}, f32[2,2,4,32,128]{4,3,2,1,0:T(8,128)S(1)}, u32[]{:S(2)}, u32[]{:S(2)}) collective-permute-start(f32[2,2,4,32,128]{4,3,2,1,0:T(8,128)S(1)} %get-tuple-element.45), channel_id=1, source_target_pairs={{0,8},{8,0},{16,24},{24,16},{1,9},{9,1},{17,25},{25,17},{2,10},{10... | collective-permute-start | bytes 786440 | tf_op jit(solution)/shard_map/ppermute | solution.py:421
  27.8 2.8 %collective-permute-done.11.z3 = f32[2,2,4,32,128]{4,3,2,1,0:T(8,128)S(1)} collective-permute-done((f32[2,2,4,32,128]{4,3,2,1,0:T(8,128)S(1)}, f32[2,2,4,32,128]{4,3,2,1,0:T(8,128)S(1)}, u32[]{:S(2)}, u32[]{:S(2)}) %collective-permute-start.11) | collective-permute-done | bytes 262176 | tf_op jit(solution)/shard_map/ppermute | solution.py:421
  30.6 1.4 %collective-permute-start.1 = (f32[2,2,4,32,128]{4,3,2,1,0:T(8,128)S(1)}, f32[2,2,4,32,128]{4,3,2,1,0:T(8,128)S(1)}, u32[]{:S(2)}, u32[]{:S(2)}) collective-permute-start(f32[2,2,4,32,128]{4,3,2,1,0:T(8,128)S(1)} %get-tuple-element.46), channel_id=1, source_target_pairs={{0,16},{8,24},{16,0},{24,8},{1,17},{9,25},{17,1},{25,9},{2,18},{10... | collective-permute-start | bytes 786440 | tf_op jit(solution)/shard_map/ppermute | solution.py:421
  32.0 0.1 gather.1
  32.0 10.0 %collective-permute-done.g1 = f32[2,2,4,32,128]{4,3,2,1,0:T(8,128)S(1)} collective-permute-done((f32[2,2,4,32,128]{4,3,2,1,0:T(8,128)S(1)}, f32[2,2,4,32,128]{4,3,2,1,0:T(8,128)S(1)}, u32[]{:S(2)}, u32[]{:S(2)}) %collective-permute-start) | collective-permute-done | bytes 262176 | tf_op jit(solution)/shard_map/ppermute | solution.py:421
  42.0 2.4 %collective-permute-start.2 = (f32[2,2,4,32,128]{4,3,2,1,0:T(8,128)S(1)}, f32[2,2,4,32,128]{4,3,2,1,0:T(8,128)S(1)}, u32[]{:S(2)}, u32[]{:S(2)}) collective-permute-start(f32[2,2,4,32,128]{4,3,2,1,0:T(8,128)S(1)} %get-tuple-element.47), channel_id=1, source_target_pairs={{0,24},{8,16},{16,8},{24,0},{1,25},{9,17},{17,9},{25,1},{2,26},{10... | collective-permute-start | bytes 786440 | tf_op jit(solution)/shard_map/ppermute | solution.py:421
  44.4 0.5 collective-permute-start.12
  45.0 0.0 collective-permute-done.4.g2
  45.0 0.5 collective-permute-start.13
  45.5 2.4 %collective-permute-start.14 = (f32[2,2,4,32,128]{4,3,2,1,0:T(8,128)S(1)}, f32[2,2,4,32,128]{4,3,2,1,0:T(8,128)S(1)}, u32[]{:S(2)}, u32[]{:S(2)}) collective-permute-start(f32[2,2,4,32,128]{4,3,2,1,0:T(8,128)S(1)} %get-tuple-element.64), channel_id=1, source_target_pairs={{0,24},{8,16},{16,8},{24,0},{1,25},{9,17},{17,9},{25,1},{2,26},{10... | collective-permute-start | bytes 786440 | tf_op jit(solution)/shard_map/ppermute | solution.py:421
  47.9 0.7 weights.1.weights_ref
  48.6 4.3 %first_rounds.2 = (s32[18,8,128]{2,1,0:T(8,128)S(1)}, s32[2,4,32,128]{3,2,1,0:T(8,128)S(1)}, f32[2,4,32,128]{3,2,1,0:T(8,128)S(1)}, f32[2,4,32,128]{3,2,1,0:T(8,128)S(1)}, f32[2,4,32,128]{3,2,1,0:T(8,128)S(1)}) custom-call(s32[88,8,128]{2,1,0:T(8,128)S(1)} %weights.1.weights_ref, f32[3,4,4,32,128]{4,3,2,1,0:T(8,128)S(1)} %get-tuple-element.48.s_ref, ...), custom_call_target="tpu_custom_call" | custom-call | tf_op jit(solution)/shard_map/first_rounds/pallas_call | solution.py:486
  52.9 0.0 collective-permute-done.1.g2
  52.9 0.5 collective-permute-start.15
  53.4 0.4 collective-permute-start.16
  53.7 4.0 %collective-permute-done.12.g1 = f32[2,2,4,32,128]{4,3,2,1,0:T(8,128)S(1)} collective-permute-done((f32[2,2,4,32,128]{4,3,2,1,0:T(8,128)S(1)}, f32[2,2,4,32,128]{4,3,2,1,0:T(8,128)S(1)}, u32[]{:S(2)}, u32[]{:S(2)}) %collective-permute-start.12) | collective-permute-done | bytes 262176 | tf_op jit(solution)/shard_map/ppermute | solution.py:421
  57.7 0.2 collective-permute-start.17
  58.0 2.2 %first_rounds.3 = (s32[18,8,128]{2,1,0:T(8,128)S(1)}, s32[2,2,32,128]{3,2,1,0:T(8,128)S(1)}, f32[2,2,32,128]{3,2,1,0:T(8,128)S(1)}, f32[2,2,32,128]{3,2,1,0:T(8,128)S(1)}, f32[2,2,32,128]{3,2,1,0:T(8,128)S(1)}) custom-call(s32[88,8,128]{2,1,0:T(8,128)S(1)} %weights.1.weights_ref, ...), custom_call_target="tpu_custom_call", output_to_operand_aliasing={{0}: (6, {})} | custom-call | tf_op jit(solution)/shard_map/first_rounds/pallas_call | solution.py:486
  60.1 0.2 collective-permute-done.15.g1
  60.3 0.5 collective-permute-start.6
  60.9 5.1 %collective-permute-done.16.g2 = f32[2,4,32,128]{3,2,1,0:T(8,128)S(1)} collective-permute-done((f32[2,4,32,128]{3,2,1,0:T(8,128)S(1)}, f32[2,4,32,128]{3,2,1,0:T(8,128)S(1)}, u32[]{:S(2)}, u32[]{:S(2)}) %collective-permute-start.16) | collective-permute-done | bytes 131104 | tf_op jit(solution)/shard_map/ppermute | solution.py:421
  66.0 0.0 collective-permute-start.7
  66.0 0.0 collective-permute-done.17.g3
  66.0 0.9 %collective-permute-start.8 = (f32[2,2,32,128]{3,2,1,0:T(8,128)S(1)}, f32[2,2,32,128]{3,2,1,0:T(8,128)S(1)}, u32[]{:S(2)}, u32[]{:S(2)}) collective-permute-start(f32[2,2,32,128]{3,2,1,0:T(8,128)S(1)} %get-tuple-element.57), channel_id=1, source_target_pairs={{0,6},{1,7},{2,4},{3,5},{4,2},{5,3},{6,0},{7,1},{8,14},{9,15},{10,... | collective-permute-start | bytes 196616 | tf_op jit(solution)/shard_map/ppermute | solution.py:421
  66.9 1.1 %shard_map.58 = (s32[18,8,128]{2,1,0:T(8,128)S(1)}, f32[3,8,32,128]{3,2,1,0:T(8,128)S(1)}, f32[3,8,32,128]{3,2,1,0:T(8,128)S(1)}) custom-call(s32[88,8,128]{2,1,0:T(8,128)S(1)} %weights.1.weights_ref, s32[2,4,32,128]{3,2,1,0:T(8,128)S(1)} %get-tuple-element.65.kept_ref, ...), custom_call_target="tpu_custom_call", output_to_operand_aliasing={{0}: (5, {})} | custom-call | tf_op jit(solution)/shard_map/pallas_call | solution.py:506
  68.0 0.0 collective-permute-done.13.g2
  68.0 2.7 %shard_map.59 = (s32[18,8,128]{2,1,0:T(8,128)S(1)}, f32[3,8,32,128]{3,2,1,0:T(8,128)S(1)}, f32[3,8,32,128]{3,2,1,0:T(8,128)S(1)}) custom-call(s32[88,8,128]{2,1,0:T(8,128)S(1)} %weights.1.weights_ref, f32[2,2,4,32,128]{4,3,2,1,0:T(8,128)S(1)} %get-tuple-element.58.z0, ...), custom_call_target="tpu_custom_call", output_to_operand_aliasing={{0}: (8, {}), {1}: (9, {}), {2}: (10, {})} | custom-call | tf_op jit(solution)/shard_map/pallas_call | solution.py:506
  70.7 0.4 collective-permute-done.7.g2
  71.2 1.0 %collective-permute-done.8.g3 = f32[2,2,32,128]{3,2,1,0:T(8,128)S(1)} collective-permute-done((f32[2,2,32,128]{3,2,1,0:T(8,128)S(1)}, f32[2,2,32,128]{3,2,1,0:T(8,128)S(1)}, u32[]{:S(2)}, u32[]{:S(2)}) %collective-permute-start.8) | collective-permute-done | bytes 65568 | tf_op jit(solution)/shard_map/ppermute | solution.py:421
  72.1 1.5 %shard_map.60 = (s32[18,8,128]{2,1,0:T(8,128)S(1)}, f32[3,8,32,128]{3,2,1,0:T(8,128)S(1)}, f32[3,8,32,128]{3,2,1,0:T(8,128)S(1)}, f32[32,1,128]{2,1,0:T(1,128)S(...) custom-call(s32[88,8,128]{2,1,0:T(8,128)S(1)} %weights.1.weights_ref, ...), custom_call_target="tpu_custom_call", output_to_operand_aliasing={{0}: (5, {}), {1}: (6, {}), {2}: (7, {})} | custom-call | tf_op jit(solution)/shard_map/pallas_call | solution.py:506
  73.6 9.8 %all_to_all.5 = f32[32,1,128]{2,1,0:T(1,128)S(1)} all-to-all(f32[32,1,128]{2,1,0:T(1,128)S(1)} %get-tuple-element.76), channel_id=1, replica_groups=mesh['gx'=4,'gy'=8] {'gx','gy'}, dimensions={0} | all-to-all | bytes 32768 | tf_op jit(solution)/shard_map/all_to_all | solution.py:571
  83.4 0.1 reduce_sum.11
  83.5 0.1 subtract_add_fusion.6
  83.6 0.1 subtract_add_fusion.5
  83.7 0.1 stack.12
  83.8 0.1 stack.14
  83.9 0.1 stack.13
  84.0 0.6 pad_maximum_fusion
  (10 shorter events, 0.1 us)
Async XLA Ops:
  6.3 14.9 %collective-permute-start.9 = (f32[2,2,4,32,128]{4,3,2,1,0:T(8,128)S(1)}, f32[2,2,4,32,128]{4,3,2,1,0:T(8,128)S(1)}, u32[]{:S(2)}, u32[]{:S(2)}) collective-permute-start(f32[2,2,4,32,128]{4,3,2,1,0:T(8,128)S(1)} %get-tuple-element.59), channel_id=1, source_target_pairs={{0,2},{1,3},{2,0},{3,1},{4,6},{5,7},{6,4},{7,5},{8,10},{9,11},{10,... | collective-permute-start | bytes 786440 | tf_op jit(solution)/shard_map/ppermute | solution.py:421
  9.4 16.9 %collective-permute-start.10 = (f32[2,2,4,32,128]{4,3,2,1,0:T(8,128)S(1)}, f32[2,2,4,32,128]{4,3,2,1,0:T(8,128)S(1)}, u32[]{:S(2)}, u32[]{:S(2)}) collective-permute-start(f32[2,2,4,32,128]{4,3,2,1,0:T(8,128)S(1)} %get-tuple-element.60), channel_id=1, source_target_pairs={{0,4},{1,5},{2,6},{3,7},{4,0},{5,1},{6,2},{7,3},{8,12},{9,13},{10,... | collective-permute-start | bytes 786440 | tf_op jit(solution)/shard_map/ppermute | solution.py:421
  12.0 32.5 %collective-permute-start.3 = (f32[2,4,4,32,128]{4,3,2,1,0:T(8,128)S(1)}, f32[2,4,4,32,128]{4,3,2,1,0:T(8,128)S(1)}, u32[]{:S(2)}, u32[]{:S(2)}) collective-permute-start(f32[2,4,4,32,128]{4,3,2,1,0:T(8,128)S(1)} %get-tuple-element.50), channel_id=1, source_target_pairs={{0,8},{8,0},{16,24},{24,16},{1,9},{9,1},{17,25},{25,17},{2,10},{10... | collective-permute-start | bytes 1572872 | tf_op jit(solution)/shard_map/ppermute | solution.py:421
  13.5 31.5 %collective-permute-start.4 = (f32[2,4,4,32,128]{4,3,2,1,0:T(8,128)S(1)}, f32[2,4,4,32,128]{4,3,2,1,0:T(8,128)S(1)}, u32[]{:S(2)}, u32[]{:S(2)}) collective-permute-start(f32[2,4,4,32,128]{4,3,2,1,0:T(8,128)S(1)} %get-tuple-element.51), channel_id=1, source_target_pairs={{0,16},{8,24},{16,0},{24,8},{1,17},{9,25},{17,1},{25,9},{2,18},{10... | collective-permute-start | bytes 1572872 | tf_op jit(solution)/shard_map/ppermute | solution.py:421
  15.0 30.5 %collective-permute-start.5 = (f32[2,4,4,32,128]{4,3,2,1,0:T(8,128)S(1)}, f32[2,4,4,32,128]{4,3,2,1,0:T(8,128)S(1)}, u32[]{:S(2)}, u32[]{:S(2)}) collective-permute-start(f32[2,4,4,32,128]{4,3,2,1,0:T(8,128)S(1)} %get-tuple-element.52), channel_id=1, source_target_pairs={{0,24},{8,16},{16,8},{24,0},{1,25},{9,17},{17,9},{25,1},{2,26},{10... | collective-permute-start | bytes 1572872 | tf_op jit(solution)/shard_map/ppermute | solution.py:421
  21.2 9.4 %collective-permute-start.11 = (f32[2,2,4,32,128]{4,3,2,1,0:T(8,128)S(1)}, f32[2,2,4,32,128]{4,3,2,1,0:T(8,128)S(1)}, u32[]{:S(2)}, u32[]{:S(2)}) collective-permute-start(f32[2,2,4,32,128]{4,3,2,1,0:T(8,128)S(1)} %get-tuple-element.61), channel_id=1, source_target_pairs={{0,6},{1,7},{2,4},{3,5},{4,2},{5,3},{6,0},{7,1},{8,14},{9,15},{10,... | collective-permute-start | bytes 786440 | tf_op jit(solution)/shard_map/ppermute | solution.py:421
  23.8 24.1 %copy-start = (s32[4]{0:T(128)S(1)}, s32[4]{0:T(128)}, u32[]{:S(2)}) copy-start(s32[4]{0:T(128)} %challenges_ref.1) | copy-start | bytes 52
  26.2 15.7 %collective-permute-start = (f32[2,2,4,32,128]{4,3,2,1,0:T(8,128)S(1)}, f32[2,2,4,32,128]{4,3,2,1,0:T(8,128)S(1)}, u32[]{:S(2)}, u32[]{:S(2)}) collective-permute-start(f32[2,2,4,32,128]{4,3,2,1,0:T(8,128)S(1)} %get-tuple-element.45), channel_id=1, source_target_pairs={{0,8},{8,0},{16,24},{24,16},{1,9},{9,1},{17,25},{25,17},{2,10},{10... | collective-permute-start | bytes 786440 | tf_op jit(solution)/shard_map/ppermute | solution.py:421
  30.6 22.3 %collective-permute-start.1 = (f32[2,2,4,32,128]{4,3,2,1,0:T(8,128)S(1)}, f32[2,2,4,32,128]{4,3,2,1,0:T(8,128)S(1)}, u32[]{:S(2)}, u32[]{:S(2)}) collective-permute-start(f32[2,2,4,32,128]{4,3,2,1,0:T(8,128)S(1)} %get-tuple-element.46), channel_id=1, source_target_pairs={{0,16},{8,24},{16,0},{24,8},{1,17},{9,25},{17,1},{25,9},{2,18},{10... | collective-permute-start | bytes 786440 | tf_op jit(solution)/shard_map/ppermute | solution.py:421
  42.0 11.4 %collective-permute-start.2 = (f32[2,2,4,32,128]{4,3,2,1,0:T(8,128)S(1)}, f32[2,2,4,32,128]{4,3,2,1,0:T(8,128)S(1)}, u32[]{:S(2)}, u32[]{:S(2)}) collective-permute-start(f32[2,2,4,32,128]{4,3,2,1,0:T(8,128)S(1)} %get-tuple-element.47), channel_id=1, source_target_pairs={{0,24},{8,16},{16,8},{24,0},{1,25},{9,17},{17,9},{25,1},{2,26},{10... | collective-permute-start | bytes 786440 | tf_op jit(solution)/shard_map/ppermute | solution.py:421
  44.4 13.3 %collective-permute-start.12 = (f32[2,2,4,32,128]{4,3,2,1,0:T(8,128)S(1)}, f32[2,2,4,32,128]{4,3,2,1,0:T(8,128)S(1)}, u32[]{:S(2)}, u32[]{:S(2)}) collective-permute-start(f32[2,2,4,32,128]{4,3,2,1,0:T(8,128)S(1)} %get-tuple-element.62), channel_id=1, source_target_pairs={{0,8},{8,0},{16,24},{24,16},{1,9},{9,1},{17,25},{25,17},{2,10},{10... | collective-permute-start | bytes 786440 | tf_op jit(solution)/shard_map/ppermute | solution.py:421
  45.0 23.0 %collective-permute-start.13 = (f32[2,2,4,32,128]{4,3,2,1,0:T(8,128)S(1)}, f32[2,2,4,32,128]{4,3,2,1,0:T(8,128)S(1)}, u32[]{:S(2)}, u32[]{:S(2)}) collective-permute-start(f32[2,2,4,32,128]{4,3,2,1,0:T(8,128)S(1)} %get-tuple-element.63), channel_id=1, source_target_pairs={{0,16},{8,24},{16,0},{24,8},{1,17},{9,25},{17,1},{25,9},{2,18},{10... | collective-permute-start | bytes 786440 | tf_op jit(solution)/shard_map/ppermute | solution.py:421
  45.5 22.5 %collective-permute-start.14 = (f32[2,2,4,32,128]{4,3,2,1,0:T(8,128)S(1)}, f32[2,2,4,32,128]{4,3,2,1,0:T(8,128)S(1)}, u32[]{:S(2)}, u32[]{:S(2)}) collective-permute-start(f32[2,2,4,32,128]{4,3,2,1,0:T(8,128)S(1)} %get-tuple-element.64), channel_id=1, source_target_pairs={{0,24},{8,16},{16,8},{24,0},{1,25},{9,17},{17,9},{25,1},{2,26},{10... | collective-permute-start | bytes 786440 | tf_op jit(solution)/shard_map/ppermute | solution.py:421
  52.9 7.4 %collective-permute-start.15 = (f32[2,4,32,128]{3,2,1,0:T(8,128)S(1)}, f32[2,4,32,128]{3,2,1,0:T(8,128)S(1)}, u32[]{:S(2)}, u32[]{:S(2)}) collective-permute-start(f32[2,4,32,128]{3,2,1,0:T(8,128)S(1)} %get-tuple-element.66), channel_id=1, source_target_pairs={{0,2},{1,3},{2,0},{3,1},{4,6},{5,7},{6,4},{7,5},{8,10},{9,11},{10,... | collective-permute-start | bytes 393224 | tf_op jit(solution)/shard_map/ppermute | solution.py:421
  53.4 12.6 %collective-permute-start.16 = (f32[2,4,32,128]{3,2,1,0:T(8,128)S(1)}, f32[2,4,32,128]{3,2,1,0:T(8,128)S(1)}, u32[]{:S(2)}, u32[]{:S(2)}) collective-permute-start(f32[2,4,32,128]{3,2,1,0:T(8,128)S(1)} %get-tuple-element.67), channel_id=1, source_target_pairs={{0,4},{1,5},{2,6},{3,7},{4,0},{5,1},{6,2},{7,3},{8,12},{9,13},{10,... | collective-permute-start | bytes 393224 | tf_op jit(solution)/shard_map/ppermute | solution.py:421
  57.7 8.3 %collective-permute-start.17 = (f32[2,4,32,128]{3,2,1,0:T(8,128)S(1)}, f32[2,4,32,128]{3,2,1,0:T(8,128)S(1)}, u32[]{:S(2)}, u32[]{:S(2)}) collective-permute-start(f32[2,4,32,128]{3,2,1,0:T(8,128)S(1)} %get-tuple-element.68), channel_id=1, source_target_pairs={{0,6},{1,7},{2,4},{3,5},{4,2},{5,3},{6,0},{7,1},{8,14},{9,15},{10,... | collective-permute-start | bytes 393224 | tf_op jit(solution)/shard_map/ppermute | solution.py:421
  60.3 10.4 %collective-permute-start.6 = (f32[2,2,32,128]{3,2,1,0:T(8,128)S(1)}, f32[2,2,32,128]{3,2,1,0:T(8,128)S(1)}, u32[]{:S(2)}, u32[]{:S(2)}) collective-permute-start(f32[2,2,32,128]{3,2,1,0:T(8,128)S(1)} %get-tuple-element.55), channel_id=1, source_target_pairs={{0,2},{1,3},{2,0},{3,1},{4,6},{5,7},{6,4},{7,5},{8,10},{9,11},{10,... | collective-permute-start | bytes 196616 | tf_op jit(solution)/shard_map/ppermute | solution.py:421
  66.0 5.2 %collective-permute-start.7 = (f32[2,2,32,128]{3,2,1,0:T(8,128)S(1)}, f32[2,2,32,128]{3,2,1,0:T(8,128)S(1)}, u32[]{:S(2)}, u32[]{:S(2)}) collective-permute-start(f32[2,2,32,128]{3,2,1,0:T(8,128)S(1)} %get-tuple-element.56), channel_id=1, source_target_pairs={{0,4},{1,5},{2,6},{3,7},{4,0},{5,1},{6,2},{7,3},{8,12},{9,13},{10,... | collective-permute-start | bytes 196616 | tf_op jit(solution)/shard_map/ppermute | solution.py:421
  66.0 6.1 %collective-permute-start.8 = (f32[2,2,32,128]{3,2,1,0:T(8,128)S(1)}, f32[2,2,32,128]{3,2,1,0:T(8,128)S(1)}, u32[]{:S(2)}, u32[]{:S(2)}) collective-permute-start(f32[2,2,32,128]{3,2,1,0:T(8,128)S(1)} %get-tuple-element.57), channel_id=1, source_target_pairs={{0,6},{1,7},{2,4},{3,5},{4,2},{5,3},{6,0},{7,1},{8,14},{9,15},{10,... | collective-permute-start | bytes 196616 | tf_op jit(solution)/shard_map/ppermute | solution.py:421

commit v3 on v2

--- a/solution.py
+++ b/solution.py
@@ -349,6 +349,15 @@
         publish_row(weights_ref, points_ref, self.sums_ref)
         for copy in self.parts[0] + self.parts[1]:
             copy.wait()
+
+
+def settle_kernel(sums_ref, out_ref):
+    total = jnp.sum(sums_ref[...], axis=0)
+    middle, highest = [pltpu.roll(total, LANES - n, 1) for n in (16, 32)]
+    for n, limb in enumerate(settle(total, middle, highest)):
+        for k in range(4):
+            row = pltpu.roll(limb, LANES - 3 * k, 1) if k else limb
+            out_ref[n, k : k + 1, :] = row[:, :3]
 
 
 def put_folded(outs, j, at, folded):
@@ -569,8 +578,14 @@
             given_raw = swap(given, "gx", gx_shift)
     sums, *folded = folded[2:]
     gathered = lax.all_to_all(sums, ("gx", "gy"), 0, 0)
-    total = gathered.sum(axis=0).reshape(LANES)
-    points = jnp.stack(settle(total[0:12], total[16:28], total[32:44])).reshape(3, 4, 3)
+    points = pl.pallas_call(
+        settle_kernel,
+        in_specs=[vmem],
+        out_specs=vmem,
+        out_shape=jax.ShapeDtypeStruct((3, 4, 3), jnp.float32),
+        compiler_params=small,
+        name="settle",
+    )(gathered)
     shape = (3, polynomials, 1, 1, row_count // 16)
     return points, folded[0].reshape(shape), folded[1].reshape(shape)
 

time: 84.7 us -> 84.4 us (level)
  other arithmetic: 0.87 us -> 0 us
where the time goes in v3:
time: 84.4 us; the launch traced here: 84.2 us
  waiting for transfers between devices  29.1 us (34%)
  starting transfers between devices  23.2 us (27%)
  Pallas kernels  21.3 us (25%)
  blocking collectives  9.85 us (12%)
    ppermute x18, waiting for transfers between devices, swap_with(): lax.ppermute(x, axis, [(i, i ^ mask) for i in range(lax.axis_size(axis))])  29.1 us
    ppermute x18, starting transfers between devices, swap_with(): lax.ppermute(x, axis, [(i, i ^ mask) for i in range(lax.axis_size(axis))])  23.2 us
    all_to_all x1, blocking collectives, shards(): gathered = lax.all_to_all(sums, ('gx', 'gy'), 0, 0)  9.85 us
    pallas_call x3, Pallas kernels, encode(): pl.pallas_call(functools.partial(encode_kernel, raw_chunk, start, owns),...  8.01 us
    pallas_call x2, Pallas kernels, first(): pl.pallas_call(functools.partial(first_kernel, fresh), in_specs=[vmem] *...  6.45 us
    pallas_call x3, Pallas kernels, fold_last(): pl.pallas_call(functools.partial(kernel, start, fresh, last), in_specs=[v...  5.32 us
  transfers between devices with their start and end apart: 18, of which 8 were waited for; matrix products, arithmetic and copies ran while one was open for 0% of the time, Pallas kernels for 16%

profile of v3, /device:TPU:0, one launch (start us, length us, event | category | flops | bytes accessed | tf_op | source)
XLA Modules:
  0.0 84.2 jit_solution(6119167978891250714)
XLA Ops:
  0.6 2.7 %encode.3 = (f32[2,4,4,32,128]{4,3,2,1,0:T(8,128)S(1)}, f32[2,4,4,32,128]{4,3,2,1,0:T(8,128)S(1)}, f32[2,4,4,32,128]{4,3,2,1,0:T(8,128)S(1)}, f32[8,128]{1,0:T(8,128)S(1)}) custom-call(f32[3,8,4,4,1,32,128]{6,5,4,3,2,1,0:T(8,128)} %bitcast.4, f32[3,8,4,4,1,32,128]{6,5,4,3,2,1,0:T(8,128)} %bitcast.7), custom_call_target="tpu_custom_call" | custom-call | tf_op jit(solution)/shard_map/encode/pallas_call | solution.py:482
  3.3 2.9 %encode.4 = (f32[2,2,4,32,128]{4,3,2,1,0:T(8,128)S(1)}, f32[2,2,4,32,128]{4,3,2,1,0:T(8,128)S(1)}, f32[2,2,4,32,128]{4,3,2,1,0:T(8,128)S(1)}, f32[2,2,4,32,128]{...) custom-call(f32[3,8,4,4,1,32,128]{6,5,4,3,2,1,0:T(8,128)} %bitcast.5, ...), custom_call_target="tpu_custom_call" | custom-call | tf_op jit(solution)/shard_map/encode/pallas_call | solution.py:482
  6.3 3.1 %collective-permute-start.9 = (f32[2,2,4,32,128]{4,3,2,1,0:T(8,128)S(1)}, f32[2,2,4,32,128]{4,3,2,1,0:T(8,128)S(1)}, u32[]{:S(2)}, u32[]{:S(2)}) collective-permute-start(f32[2,2,4,32,128]{4,3,2,1,0:T(8,128)S(1)} %get-tuple-element.59), channel_id=1, source_target_pairs={{0,2},{1,3},{2,0},{3,1},{4,6},{5,7},{6,4},{7,5},{8,10},{9,11},{10,... | collective-permute-start | bytes 786440 | tf_op jit(solution)/shard_map/ppermute | solution.py:430
  9.4 2.6 %collective-permute-start.10 = (f32[2,2,4,32,128]{4,3,2,1,0:T(8,128)S(1)}, f32[2,2,4,32,128]{4,3,2,1,0:T(8,128)S(1)}, u32[]{:S(2)}, u32[]{:S(2)}) collective-permute-start(f32[2,2,4,32,128]{4,3,2,1,0:T(8,128)S(1)} %get-tuple-element.60), channel_id=1, source_target_pairs={{0,4},{1,5},{2,6},{3,7},{4,0},{5,1},{6,2},{7,3},{8,12},{9,13},{10,... | collective-permute-start | bytes 786440 | tf_op jit(solution)/shard_map/ppermute | solution.py:430
  12.0 1.5 %collective-permute-start.3 = (f32[2,4,4,32,128]{4,3,2,1,0:T(8,128)S(1)}, f32[2,4,4,32,128]{4,3,2,1,0:T(8,128)S(1)}, u32[]{:S(2)}, u32[]{:S(2)}) collective-permute-start(f32[2,4,4,32,128]{4,3,2,1,0:T(8,128)S(1)} %get-tuple-element.50), channel_id=1, source_target_pairs={{0,8},{8,0},{16,24},{24,16},{1,9},{9,1},{17,25},{25,17},{2,10},{10... | collective-permute-start | bytes 1572872 | tf_op jit(solution)/shard_map/ppermute | solution.py:430
  13.5 1.5 %collective-permute-start.4 = (f32[2,4,4,32,128]{4,3,2,1,0:T(8,128)S(1)}, f32[2,4,4,32,128]{4,3,2,1,0:T(8,128)S(1)}, u32[]{:S(2)}, u32[]{:S(2)}) collective-permute-start(f32[2,4,4,32,128]{4,3,2,1,0:T(8,128)S(1)} %get-tuple-element.51), channel_id=1, source_target_pairs={{0,16},{8,24},{16,0},{24,8},{1,17},{9,25},{17,1},{25,9},{2,18},{10... | collective-permute-start | bytes 1572872 | tf_op jit(solution)/shard_map/ppermute | solution.py:430
  15.0 0.5 collective-permute-start.5
  15.5 5.7 %collective-permute-done.9.z1 = f32[2,2,4,32,128]{4,3,2,1,0:T(8,128)S(1)} collective-permute-done((f32[2,2,4,32,128]{4,3,2,1,0:T(8,128)S(1)}, f32[2,2,4,32,128]{4,3,2,1,0:T(8,128)S(1)}, u32[]{:S(2)}, u32[]{:S(2)}) %collective-permute-start.9) | collective-permute-done | bytes 262176 | tf_op jit(solution)/shard_map/ppermute | solution.py:430
  21.2 2.6 %collective-permute-start.11 = (f32[2,2,4,32,128]{4,3,2,1,0:T(8,128)S(1)}, f32[2,2,4,32,128]{4,3,2,1,0:T(8,128)S(1)}, u32[]{:S(2)}, u32[]{:S(2)}) collective-permute-start(f32[2,2,4,32,128]{4,3,2,1,0:T(8,128)S(1)} %get-tuple-element.61), channel_id=1, source_target_pairs={{0,6},{1,7},{2,4},{3,5},{4,2},{5,3},{6,0},{7,1},{8,14},{9,15},{10,... | collective-permute-start | bytes 786440 | tf_op jit(solution)/shard_map/ppermute | solution.py:430
  23.8 2.4 %encode.5 = (f32[2,2,4,32,128]{4,3,2,1,0:T(8,128)S(1)}, f32[2,2,4,32,128]{4,3,2,1,0:T(8,128)S(1)}, f32[2,2,4,32,128]{4,3,2,1,0:T(8,128)S(1)}, f32[8,128]{1,0:T(8,128)}) custom-call(f32[3,8,4,4,1,32,128]{6,5,4,3,2,1,0:T(8,128)} %bitcast.6, f32[3,8,4,4,1,32,128]{6,5,4,3,2,1,0:T(8,128)} %bitcast.9, f32[8,128]{1,0:T(8,128)S(1)} %get-tuple-element.44.refs_0_), custom_call_target="tpu_custom_call" | custom-call | tf_op jit(solution)/shard_map/encode/pallas_call | solution.py:482
  26.2 0.0 collective-permute-done.10.z2
  26.2 1.6 %collective-permute-start = (f32[2,2,4,32,128]{4,3,2,1,0:T(8,128)S(1)}, f32[2,2,4,32,128]{4,3,2,1,0:T(8,128)S(1)}, u32[]{:S(2)}, u32[]{:S(2)}) collective-permute-start(f32[2,2,4,32,128]{4,3,2,1,0:T(8,128)S(1)} %get-tuple-element.45), channel_id=1, source_target_pairs={{0,8},{8,0},{16,24},{24,16},{1,9},{9,1},{17,25},{25,17},{2,10},{10... | collective-permute-start | bytes 786440 | tf_op jit(solution)/shard_map/ppermute | solution.py:430
  27.8 2.8 %collective-permute-done.11.z3 = f32[2,2,4,32,128]{4,3,2,1,0:T(8,128)S(1)} collective-permute-done((f32[2,2,4,32,128]{4,3,2,1,0:T(8,128)S(1)}, f32[2,2,4,32,128]{4,3,2,1,0:T(8,128)S(1)}, u32[]{:S(2)}, u32[]{:S(2)}) %collective-permute-start.11) | collective-permute-done | bytes 262176 | tf_op jit(solution)/shard_map/ppermute | solution.py:430
  30.6 1.4 %collective-permute-start.1 = (f32[2,2,4,32,128]{4,3,2,1,0:T(8,128)S(1)}, f32[2,2,4,32,128]{4,3,2,1,0:T(8,128)S(1)}, u32[]{:S(2)}, u32[]{:S(2)}) collective-permute-start(f32[2,2,4,32,128]{4,3,2,1,0:T(8,128)S(1)} %get-tuple-element.46), channel_id=1, source_target_pairs={{0,16},{8,24},{16,0},{24,8},{1,17},{9,25},{17,1},{25,9},{2,18},{10... | collective-permute-start | bytes 786440 | tf_op jit(solution)/shard_map/ppermute | solution.py:430
  32.0 0.1 gather.1
  32.0 10.0 %collective-permute-done.g1 = f32[2,2,4,32,128]{4,3,2,1,0:T(8,128)S(1)} collective-permute-done((f32[2,2,4,32,128]{4,3,2,1,0:T(8,128)S(1)}, f32[2,2,4,32,128]{4,3,2,1,0:T(8,128)S(1)}, u32[]{:S(2)}, u32[]{:S(2)}) %collective-permute-start) | collective-permute-done | bytes 262176 | tf_op jit(solution)/shard_map/ppermute | solution.py:430
  42.0 2.4 %collective-permute-start.2 = (f32[2,2,4,32,128]{4,3,2,1,0:T(8,128)S(1)}, f32[2,2,4,32,128]{4,3,2,1,0:T(8,128)S(1)}, u32[]{:S(2)}, u32[]{:S(2)}) collective-permute-start(f32[2,2,4,32,128]{4,3,2,1,0:T(8,128)S(1)} %get-tuple-element.47), channel_id=1, source_target_pairs={{0,24},{8,16},{16,8},{24,0},{1,25},{9,17},{17,9},{25,1},{2,26},{10... | collective-permute-start | bytes 786440 | tf_op jit(solution)/shard_map/ppermute | solution.py:430
  44.4 0.0 collective-permute-done.3.g1
  44.4 0.5 collective-permute-start.12
  45.0 0.0 collective-permute-done.4.g2
  45.0 0.5 collective-permute-start.13
  45.5 0.0 collective-permute-done.5.g3
  45.5 2.4 %collective-permute-start.14 = (f32[2,2,4,32,128]{4,3,2,1,0:T(8,128)S(1)}, f32[2,2,4,32,128]{4,3,2,1,0:T(8,128)S(1)}, u32[]{:S(2)}, u32[]{:S(2)}) collective-permute-start(f32[2,2,4,32,128]{4,3,2,1,0:T(8,128)S(1)} %get-tuple-element.64), channel_id=1, source_target_pairs={{0,24},{8,16},{16,8},{24,0},{1,25},{9,17},{17,9},{25,1},{2,26},{10... | collective-permute-start | bytes 786440 | tf_op jit(solution)/shard_map/ppermute | solution.py:430
  47.9 0.7 weights.1.weights_ref
  48.6 4.3 %first_rounds.2 = (s32[18,8,128]{2,1,0:T(8,128)S(1)}, s32[2,4,32,128]{3,2,1,0:T(8,128)S(1)}, f32[2,4,32,128]{3,2,1,0:T(8,128)S(1)}, f32[2,4,32,128]{3,2,1,0:T(8,128)S(1)}, f32[2,4,32,128]{3,2,1,0:T(8,128)S(1)}) custom-call(s32[88,8,128]{2,1,0:T(8,128)S(1)} %weights.1.weights_ref, f32[3,4,4,32,128]{4,3,2,1,0:T(8,128)S(1)} %get-tuple-element.48.s_ref, ...), custom_call_target="tpu_custom_call" | custom-call | tf_op jit(solution)/shard_map/first_rounds/pallas_call | solution.py:495
  52.9 0.0 collective-permute-done.1.g2
  52.9 0.5 collective-permute-start.15
  53.4 0.0 collective-permute-done.2.g3
  53.4 0.4 collective-permute-start.16
  53.7 4.0 %collective-permute-done.12.g1 = f32[2,2,4,32,128]{4,3,2,1,0:T(8,128)S(1)} collective-permute-done((f32[2,2,4,32,128]{4,3,2,1,0:T(8,128)S(1)}, f32[2,2,4,32,128]{4,3,2,1,0:T(8,128)S(1)}, u32[]{:S(2)}, u32[]{:S(2)}) %collective-permute-start.12) | collective-permute-done | bytes 262176 | tf_op jit(solution)/shard_map/ppermute | solution.py:430
  57.7 0.2 collective-permute-start.17
  58.0 2.2 %first_rounds.3 = (s32[18,8,128]{2,1,0:T(8,128)S(1)}, s32[2,2,32,128]{3,2,1,0:T(8,128)S(1)}, f32[2,2,32,128]{3,2,1,0:T(8,128)S(1)}, f32[2,2,32,128]{3,2,1,0:T(8,128)S(1)}, f32[2,2,32,128]{3,2,1,0:T(8,128)S(1)}) custom-call(s32[88,8,128]{2,1,0:T(8,128)S(1)} %weights.1.weights_ref, ...), custom_call_target="tpu_custom_call", output_to_operand_aliasing={{0}: (6, {})} | custom-call | tf_op jit(solution)/shard_map/first_rounds/pallas_call | solution.py:495
  60.1 0.2 collective-permute-done.15.g1
  60.3 0.5 collective-permute-start.6
  60.9 5.1 %collective-permute-done.16.g2 = f32[2,4,32,128]{3,2,1,0:T(8,128)S(1)} collective-permute-done((f32[2,4,32,128]{3,2,1,0:T(8,128)S(1)}, f32[2,4,32,128]{3,2,1,0:T(8,128)S(1)}, u32[]{:S(2)}, u32[]{:S(2)}) %collective-permute-start.16) | collective-permute-done | bytes 131104 | tf_op jit(solution)/shard_map/ppermute | solution.py:430
  66.0 0.0 collective-permute-start.7
  66.0 0.0 collective-permute-done.17.g3
  66.0 0.9 %collective-permute-start.8 = (f32[2,2,32,128]{3,2,1,0:T(8,128)S(1)}, f32[2,2,32,128]{3,2,1,0:T(8,128)S(1)}, u32[]{:S(2)}, u32[]{:S(2)}) collective-permute-start(f32[2,2,32,128]{3,2,1,0:T(8,128)S(1)} %get-tuple-element.57), channel_id=1, source_target_pairs={{0,6},{1,7},{2,4},{3,5},{4,2},{5,3},{6,0},{7,1},{8,14},{9,15},{10,... | collective-permute-start | bytes 196616 | tf_op jit(solution)/shard_map/ppermute | solution.py:430
  66.9 1.1 %shard_map.58 = (s32[18,8,128]{2,1,0:T(8,128)S(1)}, f32[3,8,32,128]{3,2,1,0:T(8,128)S(1)}, f32[3,8,32,128]{3,2,1,0:T(8,128)S(1)}) custom-call(s32[88,8,128]{2,1,0:T(8,128)S(1)} %weights.1.weights_ref, s32[2,4,32,128]{3,2,1,0:T(8,128)S(1)} %get-tuple-element.65.kept_ref, ...), custom_call_target="tpu_custom_call", output_to_operand_aliasing={{0}: (5, {})} | custom-call | tf_op jit(solution)/shard_map/pallas_call | solution.py:515
  68.0 0.0 collective-permute-done.13.g2
  68.0 0.0 collective-permute-done.14.g3
  68.0 2.7 %shard_map.59 = (s32[18,8,128]{2,1,0:T(8,128)S(1)}, f32[3,8,32,128]{3,2,1,0:T(8,128)S(1)}, f32[3,8,32,128]{3,2,1,0:T(8,128)S(1)}) custom-call(s32[88,8,128]{2,1,0:T(8,128)S(1)} %weights.1.weights_ref, f32[2,2,4,32,128]{4,3,2,1,0:T(8,128)S(1)} %get-tuple-element.58.z0, ...), custom_call_target="tpu_custom_call", output_to_operand_aliasing={{0}: (8, {}), {1}: (9, {}), {2}: (10, {})} | custom-call | tf_op jit(solution)/shard_map/pallas_call | solution.py:515
  70.7 0.0 collective-permute-done.6.g1
  70.7 0.4 collective-permute-done.7.g2
  71.2 1.0 %collective-permute-done.8.g3 = f32[2,2,32,128]{3,2,1,0:T(8,128)S(1)} collective-permute-done((f32[2,2,32,128]{3,2,1,0:T(8,128)S(1)}, f32[2,2,32,128]{3,2,1,0:T(8,128)S(1)}, u32[]{:S(2)}, u32[]{:S(2)}) %collective-permute-start.8) | collective-permute-done | bytes 65568 | tf_op jit(solution)/shard_map/ppermute | solution.py:430
  72.1 1.5 %shard_map.60 = (s32[18,8,128]{2,1,0:T(8,128)S(1)}, f32[3,8,32,128]{3,2,1,0:T(8,128)S(1)}, f32[3,8,32,128]{3,2,1,0:T(8,128)S(1)}, f32[32,1,128]{2,1,0:T(1,128)S(...) custom-call(s32[88,8,128]{2,1,0:T(8,128)S(1)} %weights.1.weights_ref, ...), custom_call_target="tpu_custom_call", output_to_operand_aliasing={{0}: (5, {}), {1}: (6, {}), {2}: (7, {})} | custom-call | tf_op jit(solution)/shard_map/pallas_call | solution.py:515
  73.6 9.8 %all_to_all.5.sums_ref = f32[32,1,128]{2,1,0:T(1,128)S(1)} all-to-all(f32[32,1,128]{2,1,0:T(1,128)S(1)} %get-tuple-element.76), channel_id=1, replica_groups=mesh['gx'=4,'gy'=8] {'gx','gy'}, dimensions={0} | all-to-all | bytes 32768 | tf_op jit(solution)/shard_map/all_to_all | solution.py:580
  83.4 0.8 settle.1
  (2 shorter events, 0.0 us)
Async XLA Ops:
  6.3 14.9 %collective-permute-start.9 = (f32[2,2,4,32,128]{4,3,2,1,0:T(8,128)S(1)}, f32[2,2,4,32,128]{4,3,2,1,0:T(8,128)S(1)}, u32[]{:S(2)}, u32[]{:S(2)}) collective-permute-start(f32[2,2,4,32,128]{4,3,2,1,0:T(8,128)S(1)} %get-tuple-element.59), channel_id=1, source_target_pairs={{0,2},{1,3},{2,0},{3,1},{4,6},{5,7},{6,4},{7,5},{8,10},{9,11},{10,... | collective-permute-start | bytes 786440 | tf_op jit(solution)/shard_map/ppermute | solution.py:430
  9.4 16.9 %collective-permute-start.10 = (f32[2,2,4,32,128]{4,3,2,1,0:T(8,128)S(1)}, f32[2,2,4,32,128]{4,3,2,1,0:T(8,128)S(1)}, u32[]{:S(2)}, u32[]{:S(2)}) collective-permute-start(f32[2,2,4,32,128]{4,3,2,1,0:T(8,128)S(1)} %get-tuple-element.60), channel_id=1, source_target_pairs={{0,4},{1,5},{2,6},{3,7},{4,0},{5,1},{6,2},{7,3},{8,12},{9,13},{10,... | collective-permute-start | bytes 786440 | tf_op jit(solution)/shard_map/ppermute | solution.py:430
  12.0 32.5 %collective-permute-start.3 = (f32[2,4,4,32,128]{4,3,2,1,0:T(8,128)S(1)}, f32[2,4,4,32,128]{4,3,2,1,0:T(8,128)S(1)}, u32[]{:S(2)}, u32[]{:S(2)}) collective-permute-start(f32[2,4,4,32,128]{4,3,2,1,0:T(8,128)S(1)} %get-tuple-element.50), channel_id=1, source_target_pairs={{0,8},{8,0},{16,24},{24,16},{1,9},{9,1},{17,25},{25,17},{2,10},{10... | collective-permute-start | bytes 1572872 | tf_op jit(solution)/shard_map/ppermute | solution.py:430
  13.5 31.5 %collective-permute-start.4 = (f32[2,4,4,32,128]{4,3,2,1,0:T(8,128)S(1)}, f32[2,4,4,32,128]{4,3,2,1,0:T(8,128)S(1)}, u32[]{:S(2)}, u32[]{:S(2)}) collective-permute-start(f32[2,4,4,32,128]{4,3,2,1,0:T(8,128)S(1)} %get-tuple-element.51), channel_id=1, source_target_pairs={{0,16},{8,24},{16,0},{24,8},{1,17},{9,25},{17,1},{25,9},{2,18},{10... | collective-permute-start | bytes 1572872 | tf_op jit(solution)/shard_map/ppermute | solution.py:430
  15.0 30.5 %collective-permute-start.5 = (f32[2,4,4,32,128]{4,3,2,1,0:T(8,128)S(1)}, f32[2,4,4,32,128]{4,3,2,1,0:T(8,128)S(1)}, u32[]{:S(2)}, u32[]{:S(2)}) collective-permute-start(f32[2,4,4,32,128]{4,3,2,1,0:T(8,128)S(1)} %get-tuple-element.52), channel_id=1, source_target_pairs={{0,24},{8,16},{16,8},{24,0},{1,25},{9,17},{17,9},{25,1},{2,26},{10... | collective-permute-start | bytes 1572872 | tf_op jit(solution)/shard_map/ppermute | solution.py:430
  21.2 9.4 %collective-permute-start.11 = (f32[2,2,4,32,128]{4,3,2,1,0:T(8,128)S(1)}, f32[2,2,4,32,128]{4,3,2,1,0:T(8,128)S(1)}, u32[]{:S(2)}, u32[]{:S(2)}) collective-permute-start(f32[2,2,4,32,128]{4,3,2,1,0:T(8,128)S(1)} %get-tuple-element.61), channel_id=1, source_target_pairs={{0,6},{1,7},{2,4},{3,5},{4,2},{5,3},{6,0},{7,1},{8,14},{9,15},{10,... | collective-permute-start | bytes 786440 | tf_op jit(solution)/shard_map/ppermute | solution.py:430
  23.8 24.1 %copy-start = (s32[4]{0:T(128)S(1)}, s32[4]{0:T(128)}, u32[]{:S(2)}) copy-start(s32[4]{0:T(128)} %challenges_ref.1) | copy-start | bytes 52
  26.2 15.7 %collective-permute-start = (f32[2,2,4,32,128]{4,3,2,1,0:T(8,128)S(1)}, f32[2,2,4,32,128]{4,3,2,1,0:T(8,128)S(1)}, u32[]{:S(2)}, u32[]{:S(2)}) collective-permute-start(f32[2,2,4,32,128]{4,3,2,1,0:T(8,128)S(1)} %get-tuple-element.45), channel_id=1, source_target_pairs={{0,8},{8,0},{16,24},{24,16},{1,9},{9,1},{17,25},{25,17},{2,10},{10... | collective-permute-start | bytes 786440 | tf_op jit(solution)/shard_map/ppermute | solution.py:430
  30.6 22.3 %collective-permute-start.1 = (f32[2,2,4,32,128]{4,3,2,1,0:T(8,128)S(1)}, f32[2,2,4,32,128]{4,3,2,1,0:T(8,128)S(1)}, u32[]{:S(2)}, u32[]{:S(2)}) collective-permute-start(f32[2,2,4,32,128]{4,3,2,1,0:T(8,128)S(1)} %get-tuple-element.46), channel_id=1, source_target_pairs={{0,16},{8,24},{16,0},{24,8},{1,17},{9,25},{17,1},{25,9},{2,18},{10... | collective-permute-start | bytes 786440 | tf_op jit(solution)/shard_map/ppermute | solution.py:430
  42.0 11.4 %collective-permute-start.2 = (f32[2,2,4,32,128]{4,3,2,1,0:T(8,128)S(1)}, f32[2,2,4,32,128]{4,3,2,1,0:T(8,128)S(1)}, u32[]{:S(2)}, u32[]{:S(2)}) collective-permute-start(f32[2,2,4,32,128]{4,3,2,1,0:T(8,128)S(1)} %get-tuple-element.47), channel_id=1, source_target_pairs={{0,24},{8,16},{16,8},{24,0},{1,25},{9,17},{17,9},{25,1},{2,26},{10... | collective-permute-start | bytes 786440 | tf_op jit(solution)/shard_map/ppermute | solution.py:430
  44.4 13.3 %collective-permute-start.12 = (f32[2,2,4,32,128]{4,3,2,1,0:T(8,128)S(1)}, f32[2,2,4,32,128]{4,3,2,1,0:T(8,128)S(1)}, u32[]{:S(2)}, u32[]{:S(2)}) collective-permute-start(f32[2,2,4,32,128]{4,3,2,1,0:T(8,128)S(1)} %get-tuple-element.62), channel_id=1, source_target_pairs={{0,8},{8,0},{16,24},{24,16},{1,9},{9,1},{17,25},{25,17},{2,10},{10... | collective-permute-start | bytes 786440 | tf_op jit(solution)/shard_map/ppermute | solution.py:430
  45.0 23.0 %collective-permute-start.13 = (f32[2,2,4,32,128]{4,3,2,1,0:T(8,128)S(1)}, f32[2,2,4,32,128]{4,3,2,1,0:T(8,128)S(1)}, u32[]{:S(2)}, u32[]{:S(2)}) collective-permute-start(f32[2,2,4,32,128]{4,3,2,1,0:T(8,128)S(1)} %get-tuple-element.63), channel_id=1, source_target_pairs={{0,16},{8,24},{16,0},{24,8},{1,17},{9,25},{17,1},{25,9},{2,18},{10... | collective-permute-start | bytes 786440 | tf_op jit(solution)/shard_map/ppermute | solution.py:430
  45.5 22.5 %collective-permute-start.14 = (f32[2,2,4,32,128]{4,3,2,1,0:T(8,128)S(1)}, f32[2,2,4,32,128]{4,3,2,1,0:T(8,128)S(1)}, u32[]{:S(2)}, u32[]{:S(2)}) collective-permute-start(f32[2,2,4,32,128]{4,3,2,1,0:T(8,128)S(1)} %get-tuple-element.64), channel_id=1, source_target_pairs={{0,24},{8,16},{16,8},{24,0},{1,25},{9,17},{17,9},{25,1},{2,26},{10... | collective-permute-start | bytes 786440 | tf_op jit(solution)/shard_map/ppermute | solution.py:430
  52.9 7.4 %collective-permute-start.15 = (f32[2,4,32,128]{3,2,1,0:T(8,128)S(1)}, f32[2,4,32,128]{3,2,1,0:T(8,128)S(1)}, u32[]{:S(2)}, u32[]{:S(2)}) collective-permute-start(f32[2,4,32,128]{3,2,1,0:T(8,128)S(1)} %get-tuple-element.66), channel_id=1, source_target_pairs={{0,2},{1,3},{2,0},{3,1},{4,6},{5,7},{6,4},{7,5},{8,10},{9,11},{10,... | collective-permute-start | bytes 393224 | tf_op jit(solution)/shard_map/ppermute | solution.py:430
  53.4 12.6 %collective-permute-start.16 = (f32[2,4,32,128]{3,2,1,0:T(8,128)S(1)}, f32[2,4,32,128]{3,2,1,0:T(8,128)S(1)}, u32[]{:S(2)}, u32[]{:S(2)}) collective-permute-start(f32[2,4,32,128]{3,2,1,0:T(8,128)S(1)} %get-tuple-element.67), channel_id=1, source_target_pairs={{0,4},{1,5},{2,6},{3,7},{4,0},{5,1},{6,2},{7,3},{8,12},{9,13},{10,... | collective-permute-start | bytes 393224 | tf_op jit(solution)/shard_map/ppermute | solution.py:430
  57.7 8.3 %collective-permute-start.17 = (f32[2,4,32,128]{3,2,1,0:T(8,128)S(1)}, f32[2,4,32,128]{3,2,1,0:T(8,128)S(1)}, u32[]{:S(2)}, u32[]{:S(2)}) collective-permute-start(f32[2,4,32,128]{3,2,1,0:T(8,128)S(1)} %get-tuple-element.68), channel_id=1, source_target_pairs={{0,6},{1,7},{2,4},{3,5},{4,2},{5,3},{6,0},{7,1},{8,14},{9,15},{10,... | collective-permute-start | bytes 393224 | tf_op jit(solution)/shard_map/ppermute | solution.py:430
  60.3 10.4 %collective-permute-start.6 = (f32[2,2,32,128]{3,2,1,0:T(8,128)S(1)}, f32[2,2,32,128]{3,2,1,0:T(8,128)S(1)}, u32[]{:S(2)}, u32[]{:S(2)}) collective-permute-start(f32[2,2,32,128]{3,2,1,0:T(8,128)S(1)} %get-tuple-element.55), channel_id=1, source_target_pairs={{0,2},{1,3},{2,0},{3,1},{4,6},{5,7},{6,4},{7,5},{8,10},{9,11},{10,... | collective-permute-start | bytes 196616 | tf_op jit(solution)/shard_map/ppermute | solution.py:430
  66.0 5.2 %collective-permute-start.7 = (f32[2,2,32,128]{3,2,1,0:T(8,128)S(1)}, f32[2,2,32,128]{3,2,1,0:T(8,128)S(1)}, u32[]{:S(2)}, u32[]{:S(2)}) collective-permute-start(f32[2,2,32,128]{3,2,1,0:T(8,128)S(1)} %get-tuple-element.56), channel_id=1, source_target_pairs={{0,4},{1,5},{2,6},{3,7},{4,0},{5,1},{6,2},{7,3},{8,12},{9,13},{10,... | collective-permute-start | bytes 196616 | tf_op jit(solution)/shard_map/ppermute | solution.py:430
  66.0 6.1 %collective-permute-start.8 = (f32[2,2,32,128]{3,2,1,0:T(8,128)S(1)}, f32[2,2,32,128]{3,2,1,0:T(8,128)S(1)}, u32[]{:S(2)}, u32[]{:S(2)}) collective-permute-start(f32[2,2,32,128]{3,2,1,0:T(8,128)S(1)} %get-tuple-element.57), channel_id=1, source_target_pairs={{0,6},{1,7},{2,4},{3,5},{4,2},{5,3},{6,0},{7,1},{8,14},{9,15},{10,... | collective-permute-start | bytes 196616 | tf_op jit(solution)/shard_map/ppermute | solution.py:430
